TPU v7x, 256 devices: a whole 4x4x8 slice. The times are simulated.
256 devices in a mesh: sens: 8 (over z_lo, core), pts: 32 (over y, z_hi, x).
Axes of the slice: x: 4, y: 4, z: 8 (z_hi: 2, z_lo: 4; z = z_hi * 4 + z_lo), core: 2. Of those that a mesh axis runs over, the one named last changes fastest.
Arguments:
- kernel: float32 [64, 2048, 384], P('sens', 'pts'), may hold values from -0.0068359375 to 0.0068359375
- vectors: float32 [8, 2048, 384], P(None, 'pts'), may hold values from -6 to 6
- noise_scale: float32 [64], P('sens'), may hold values from 0.5 to 2
- sensor_group: int32 [64], P('sens'), may hold values from 0 to 3
- correlation: float32 [4, 384, 384], replicated, may hold values from -0.3125 to 0.3125
- stiffness: float32 [2048], P('pts'), may hold values from 0.2 to 1
- couplings: float32 [4, 2048], P(None, 'pts'), may hold values from 0.05 to 0.5
- neighbors: int32 [4, 2048], P(None, 'pts'), may hold values from 0 to 2047, as said below
Outputs:
- hessian_action: float32 [8, 2048, 384], P('sens', 'pts')
Inputs may be any that keep to these rules, and one draw needn't show every extreme that they name: `neighbors`: points are numbered row by row on a grid of rows of 16 points; every neighbor of point p lies in p's grid row or in one of the two rows beside it.
All inputs are finite; a program needn't handle non-finite values.
Results may differ from a plain program's by a relative error of at most 0.0001.
Values sent between devices are 32-bit elements; how exact they have to be, the bound alone decides.
A program may use at most 64 MiB of HBM per device.

v0:
```python
import math

import jax
import jax.numpy as jnp
from jax import lax
from jax.sharding import PartitionSpec as P

COLS = 16


HIGHEST = lax.Precision.HIGHEST


def padded_2(block, sides, width):
    for axis, dim in sides:
        count = lax.axis_size(axis)
        forward = [(i, i + 1) for i in range(count - 1)]
        backward = [(target, source) for source, target in forward]
        low = lax.ppermute(
            lax.slice_in_dim(block, block.shape[dim] - width, None, axis=dim), axis, forward
        )
        high = lax.ppermute(lax.slice_in_dim(block, 0, width, axis=dim), axis, backward)
        block = jnp.concatenate([low, block, high], axis=dim)
    return block


def tables(length):
    span = 2 * length
    steps = lax.iota(jnp.int32, length)
    phase = steps[:, None] * steps[None, :] % span
    angle = phase.astype(jnp.float32) * (2.0 * math.pi / span)
    cosine = jnp.cos(angle)
    sine = jnp.sin(angle)
    nyquist = jnp.where(steps % 2 == 0, 1.0, -1.0).astype(jnp.float32)
    first_col = steps == 0
    second = jnp.where(first_col[None, :], nyquist[:, None], -sine)
    forward = jnp.concatenate([cosine, second], axis=1)
    weight = jnp.where(first_col, 1.0, 2.0).astype(jnp.float32)
    back_first = cosine * weight[:, None]
    back_second = jnp.where(first_col[:, None], nyquist[None, :], -2.0 * sine)
    inverse = jnp.concatenate([back_first, back_second], axis=0) / span
    return (forward, inverse)


def spectral(left, right, form, half):
    left_x, left_y = (left[..., :half], left[..., half:])
    right_x, right_y = (right[..., :half], right[..., half:])
    prod_xx = jnp.einsum(form, left_x, right_x, precision=HIGHEST)
    prod_yy = jnp.einsum(form, left_y, right_y, precision=HIGHEST)
    prod_xy = jnp.einsum(form, left_x, right_y, precision=HIGHEST)
    prod_yx = jnp.einsum(form, left_y, right_x, precision=HIGHEST)
    keep = (lax.iota(jnp.int32, half) > 0).astype(jnp.float32)
    real_part = prod_xx - keep * prod_yy
    imag_part = keep * (prod_xy + prod_yx) + (1.0 - keep) * prod_yy
    return jnp.concatenate([real_part, imag_part], axis=-1)


def weight_rows(rows, row_ids, noise_scale, sensor_group, correlation):
    sensors = noise_scale.shape[0]
    groups = correlation.shape[0]
    pick = (row_ids[:, None] % sensors == lax.iota(jnp.int32, sensors)[None, :]).astype(jnp.float32)
    group_table = (sensor_group[:, None] == lax.iota(jnp.int32, groups)[None, :]).astype(
        jnp.float32
    )
    row_scale = jnp.dot(pick, noise_scale, precision=HIGHEST)
    row_group = jnp.dot(pick, group_table, precision=HIGHEST)
    mixed = jnp.einsum("rt,but->rbu", rows, correlation, precision=HIGHEST)
    extra = jnp.einsum("rbu,rb->ru", mixed, row_group, precision=HIGHEST)
    return row_scale[:, None] * (rows + extra)


def local(kernel, vectors, noise_scale, sensor_group, correlation, stiffness, couplings, neighbors):
    sensors, points, length = kernel.shape
    count = vectors.shape[0]
    forward, inverse = tables(length)
    kern_hat = jnp.einsum("spt,tf->spf", kernel, forward, precision=HIGHEST)
    vec_hat = jnp.einsum("kpt,tf->kpf", vectors, forward, precision=HIGHEST)
    pred_hat = spectral(vec_hat, kern_hat, "kpf,spf->ksf", length)
    partial_value = jnp.einsum("ksf,ft->kst", pred_hat, inverse, precision=HIGHEST)
    flat = partial_value.reshape(count * sensors, length)
    predicted = lax.psum(flat, "pts")
    row_ids = lax.iota(jnp.int32, count * sensors)
    weighted = weight_rows(predicted, row_ids, noise_scale, sensor_group, correlation)
    residual = weighted.reshape(count, sensors, length)
    res_hat = jnp.einsum("kst,tf->ksf", residual, forward, precision=HIGHEST)
    columns = lax.iota(jnp.int32, 2 * length)
    flip = jnp.where(columns > length, -1.0, 1.0).astype(jnp.float32)
    conj_hat = kern_hat * flip
    grad_hat = spectral(res_hat, conj_hat, "ksf,spf->kpf", length)
    own_count = count // lax.axis_size("sens")
    data_term = lax.psum_scatter(
        jnp.einsum("kpf,ft->kpt", grad_hat, inverse, precision=HIGHEST),
        "sens",
        scatter_dimension=0,
        tiled=True,
    )
    own_vectors = lax.dynamic_slice_in_dim(
        vectors, lax.axis_index("sens") * own_count, own_count, 0
    )
    padded = padded_2(own_vectors, (("pts", 1),), COLS)
    local_index = neighbors - lax.axis_index("pts") * points + COLS
    gathered = jnp.take(padded, local_index, axis=1)
    prior_term = stiffness[None, :, None] * own_vectors
    prior_term = prior_term + jnp.sum(
        couplings[None, :, :, None] * (own_vectors[:, None] - gathered), axis=1
    )
    return data_term + prior_term


def solution(mesh):
    in_specs = (
        P("sens", "pts", None),
        P(None, "pts", None),
        P("sens"),
        P("sens"),
        P(),
        P("pts"),
        P(None, "pts"),
        P(None, "pts"),
    )
    out_specs = P("sens", "pts", None)
    return jax.shard_map(local, mesh=mesh, in_specs=in_specs, out_specs=out_specs, check_vma=False)
```

profile of v0, /device:TPU:1, one launch (start us, length us, event | category | flops | bytes accessed | tf_op | source)
XLA Modules:
  0.0 535.4 jit_solution(15899717636893823764)
XLA Ops:
  6.6 2.2 fusion.13
  8.8 3.3 multiply_select_fusion
  12.2 2.7 broadcast_multiply_fusion
  14.9 1.7 fusion.47
  16.7 2.8 copy.15
  19.4 3.8 convolution_bitcast_fusion
  23.2 1.4 fusion.49
  24.6 2.8 copy.16
  27.4 2.8 copy.23
  30.2 5.9 %fusion.51 = f32[384,8,8]{2,1,0:T(8,128)} fusion(f32[8,64,384]{1,0,2:T(8,128)} %copy.15, f32[8,64,384]{1,0,2:T(8,128)} %copy.16), kind=kOutput, calls=%fused_computation.86 | convolution fusion | flops 18874368 | bytes 1671168 | tf_op jit(solution)/shard_map/kpf,spf->ksf/dot_general | solution.py:49
  36.1 4.0 fusion.52
  40.1 2.9 copy.22
  43.0 6.4 %subtract_bitcast_fusion.1 = f32[8,8,384]{0,1,2:T(8,128)} fusion(f32[384,8,8]{2,1,0:T(8,128)} %fusion.51, f32[8,64,384]{1,0,2:T(8,128)} %copy.22, f32[8,64,384]{1,0,2:T(8,128)} %copy.23, f32[384]{0:T(512)S(1)} %fusion.38), kind=kOutput, calls=%fused_computation.7 | convolution fusion | flops 18923520 | bytes 1771008 | tf_op jit(solution)/shard_map/kpf,spf->ksf/dot_general | solution.py:48
  49.4 4.4 add_bitcast_fusion.1
  53.8 2.5 copy.18
  56.2 2.5 copy.17
  58.7 2.3 broadcast_multiply_fusion.1
  61.0 0.8 copy-done.11
  61.8 2.6 convolution_bitcast_fusion.2
  64.4 0.4 reduce-scatter.2.cloned.1.call-start
  64.9 0.6 and_select_fusion
  65.5 2.8 copy.19
  68.3 2.8 copy.27
  71.1 1.5 fusion.28
  72.5 0.8 convolution_bitcast_fusion.3
  73.4 376.9 %all-reduce.2.cloned.1.call-done = f32[64,384]{1,0:T(8,128)} async-done(((f32[64,384]{1,0:T(8,128)}), f32[64,384]{1,0:T(8,128)}) %all-reduce.2.cloned.1.call-update) | async-done | bytes 98320 | tf_op jit(solution)/shard_map/psum | solution.py:81
  450.3 3.4 fusion.24
  453.7 1.2 fusion.15
  454.9 0.8 fusion.5
  455.8 1.7 copy.29
  457.4 1.7 copy.28
  459.1 5.4 %fusion.53 = f32[384,64,8]{1,2,0:T(8,128)S(1)} fusion(f32[8,64,384]{1,0,2:T(8,128)} %copy.19, f32[8,8,384]{0,1,2:T(8,128)} %copy.29), kind=kOutput, calls=%fused_computation.88 | convolution fusion | flops 18874368 | bytes 1671168 | tf_op jit(solution)/shard_map/ksf,spf->kpf/dot_general | solution.py:49
  464.5 3.5 fusion.54
  468.1 3.6 subtract_bitcast_fusion
  471.7 4.2 add_bitcast_fusion
  475.9 0.2 pad_maximum_fusion
  476.1 0.8 copy-done.12
  476.9 0.2 copy-done.13
  477.1 6.6 %fusion = f32[8,64,384]{2,1,0:T(8,128)} fusion(f32[8,64,768]{1,0,2:T(8,128)S(1)} %pad_maximum_fusion, f32[384,384]{1,0:T(8,128)S(1)} %copy-done.13, f32[384,384]{1,0:T(8,128)S(1)} %copy-done.12), kind=kOutput, calls=%fused_computation.2 | convolution fusion | flops 1812529152 | bytes 3538944 | tf_op jit(solution)/shard_map/kpf,ft->kpt/dot_general | solution.py:92
  483.7 0.8 constant_dynamic-slice_fusion.1
  484.5 1.3 collective-permute-start
  485.8 1.3 collective-permute-start.1
  487.2 0.9 constant_dynamic-slice_fusion.2
  488.1 0.9 fusion.75
  489.0 1.3 collective-permute-done.1
  490.4 1.0 gather_fusion
  491.5 35.2 %reduce-scatter.2.cloned.1.call-done = f32[1,64,384]{2,1,0:T(8,128)} async-done(((f32[8,64,384]{2,1,0:T(8,128)}), f32[1,64,384]{2,1,0:T(8,128)}) %reduce-scatter.2.cloned.1.call-update) | async-done | bytes 98320 | tf_op jit(solution)/shard_map/reduce_scatter | solution.py:91
  526.8 1.7 fusion.20
  (57 shorter events, 0.4 us)
Async XLA Ops:
  6.5 443.7 %copy-start = (f32[4,384,384]{2,1,0:T(8,128)S(1)}, f32[4,384,384]{2,1,0:T(8,128)}, u32[]{:S(2)}) copy-start(f32[4,384,384]{2,1,0:T(8,128)} %param.12) | copy-start | bytes 7077892
  6.5 443.7 %all-reduce.2.cloned.1.call-start = ((), (), s32[]{:S(2)}) async-start(), calls=%async_computation.1 | async-start | bytes 196608 | tf_op jit(solution)/shard_map/psum | solution.py:81
  6.5 5.6 %copy-start.14 = (f32[8,64,384]{2,1,0:T(8,128)S(1)}, f32[8,64,384]{2,1,0:T(8,128)}, u32[]{:S(2)}) copy-start(f32[8,64,384]{2,1,0:T(8,128)} %param.8) | copy-start | bytes 2359300
  30.2 5.9 %copy-start.7 = (f32[8,64,384]{1,0,2:T(8,128)S(1)}, f32[8,64,384]{1,0,2:T(8,128)}, u32[]{:S(2)}) copy-start(f32[8,64,384]{1,0,2:T(8,128)} %copy.15) | copy-start | bytes 2359300
  30.2 5.9 %copy-start.8 = (f32[8,64,384]{1,0,2:T(8,128)S(1)}, f32[8,64,384]{1,0,2:T(8,128)}, u32[]{:S(2)}) copy-start(f32[8,64,384]{1,0,2:T(8,128)} %copy.23) | copy-start | bytes 2359300
  42.9 6.4 %copy-start.3 = (f32[8,64,384]{1,0,2:T(8,128)S(1)}, f32[8,64,384]{1,0,2:T(8,128)}, u32[]{:S(2)}) copy-start(f32[8,64,384]{1,0,2:T(8,128)} %copy.16) | copy-start | bytes 2359300
  43.0 6.4 %copy-start.4 = (f32[384,8,8]{2,1,0:T(8,128)S(1)}, f32[384,8,8]{2,1,0:T(8,128)}, u32[]{:S(2)}) copy-start(f32[384,8,8]{2,1,0:T(8,128)} %fusion.51) | copy-start | bytes 294916
  43.0 6.4 %copy-start.5 = (f32[8,64,384]{1,0,2:T(8,128)S(1)}, f32[8,64,384]{1,0,2:T(8,128)}, u32[]{:S(2)}) copy-start(f32[8,64,384]{1,0,2:T(8,128)} %copy.22) | copy-start | bytes 2359300
  43.0 6.4 %copy-start.10 = (f32[384,8,8]{2,1,0:T(8,128)S(1)}, f32[384,8,8]{2,1,0:T(8,128)}, u32[]{:S(2)}) copy-start(f32[384,8,8]{2,1,0:T(8,128)} %fusion.52) | copy-start | bytes 294916
  61.0 0.8 copy-start.11
  64.4 462.3 %reduce-scatter.2.cloned.1.call-start = ((), (), s32[]{:S(2)}) async-start(), calls=%async_computation.2 | async-start | bytes 884736 | tf_op jit(solution)/shard_map/reduce_scatter | solution.py:91
  68.3 2.8 copy-start.20
  68.3 4.3 copy-start.21
  450.3 3.4 copy-start.16
  450.3 4.6 copy-start.15
  459.1 5.4 %copy-start.6 = (f32[8,64,384]{1,0,2:T(8,128)S(1)}, f32[8,64,384]{1,0,2:T(8,128)}, u32[]{:S(2)}) copy-start(f32[8,64,384]{1,0,2:T(8,128)} %copy.19) | copy-start | bytes 2359300
  459.1 5.4 %copy-start.9 = (f32[8,8,384]{0,1,2:T(8,128)S(1)}, f32[8,8,384]{0,1,2:T(8,128)}, u32[]{:S(2)}) copy-start(f32[8,8,384]{0,1,2:T(8,128)} %copy.28) | copy-start | bytes 294916
  464.5 3.5 copy-start.1
  468.0 3.6 copy-start.2
  475.8 1.1 copy-start.12
  475.8 1.2 copy-start.13
  477.1 10.0 %copy-start.18 = (s32[4,64]{1,0:T(4,128)S(1)}, s32[4,64]{1,0:T(4,128)}, u32[]{:S(2)}) copy-start(s32[4,64]{1,0:T(4,128)} %param.15) | copy-start | bytes 3076
  484.5 4.5 collective-permute-start
  485.8 4.6 collective-permute-start.1
  490.4 1.0 copy-start.17
  490.4 36.4 %copy-start.19 = (f32[64]{0:T(128)S(1)}, f32[64]{0:T(128)}, u32[]{:S(2)}) copy-start(f32[64]{0:T(128)} %param.13) | copy-start | bytes 772
Sparse Core Ops, SparseCore 0:
  64.6 385.6 all-reduce.1
  483.8 42.8 reduce-scatter.1
where the time goes:
time: 541 us; the launch traced here: 535 us
  waiting for transfers between devices  413 us (76%)
  matrix products  60.8 us (11%)
  local copies, waits for them, and re-layouts  33.8 us (6%)
  between operations  13.9 us (3%)
  other arithmetic  10.4 us (2%)
    psum x1, waiting for transfers between devices, local(): predicted = lax.psum(flat, 'pts')  377 us
    reduce_scatter x1, waiting for transfers between devices, local(): lax.psum_scatter(jnp.einsum('kpf,ft->kpt', grad_hat, inverse, precision=H...  35.2 us
    slice x5, local copies, waits for them, and re-layouts, spectral(): right_x, right_y = (right[..., :half], right[..., half:])  13 us
    dot_general x2, matrix products, spectral(): prod_yy = jnp.einsum(form, left_y, right_y, precision=HIGHEST)  11.2 us
  transfers between devices with their start and end apart: 4, of which 3 were waited for; matrix products, arithmetic and copies ran while one was open for 2% of the time, Pallas kernels for 0%

commit v1 on v0

v1 whole, which is shorter than its diff:
```python
import functools
import math

import jax
import jax.numpy as jnp
import numpy as np
from jax import lax
from jax.experimental import pallas as pl
from jax.experimental.pallas import tpu as pltpu
from jax.sharding import PartitionSpec as P

F32, BF16 = jnp.float32, jnp.bfloat16
K, NT, NB, SD, PD, COLS = 8, 384, 4, 8, 64, 16
F2 = 2 * NT
LANES = 128
FT = NT // LANES
PLANE = sorted(
    ((dx, dy) for dx in range(4) for dy in range(4) if dx or dy),
    key=lambda d: -(min(d[0], 4 - d[0]) + min(d[1], 4 - d[1])),
)


def table():
    t = np.arange(NT)
    angle = 2.0 * math.pi / F2 * (t[:, None] * t[None, :] % F2)
    second = -np.sin(angle)
    second[:, 0] = np.where(t % 2 == 0, 1.0, -1.0)
    full = np.concatenate([np.cos(angle), second], axis=1).astype(np.float32)
    high = full.astype(BF16)
    low = (full - high.astype(np.float32)).astype(BF16)
    return high, low


def split(x):
    high = x.astype(BF16)
    low = (x - high.astype(F32)).astype(BF16)
    return high, low


def stack(x):
    high, low = split(x)
    return jnp.concatenate([high, low, high], axis=1)


def matmul(a, b):
    return lax.dot_general(a, b, (((1,), (0,)), ((), ())), preferred_element_type=F32)


def matmul_t(a, b):
    return lax.dot_general(a, b, (((1,), (1,)), ((), ())), preferred_element_type=F32)


def body(
    kern_hbm, vec_hbm, noise, group, corr_hbm, stiff_hbm, coup_hbm, nbr_hbm, fh_hbm, fl_hbm,
    out_ref,
    kern, vec, corr, stiff, coup, nbr, fh, fl,
    kh, km, vh, ph, part, rs_in, zsum, z_in, mine, resid, rh, grad, prior,
    halo_lo, halo_hi, core_out, core_in, line_out, line_in,
    load_sem, halo_send, halo_recv, rs_send, rs_recv, z_send, z_recv, ag_send, ag_recv,
    core_send, core_recv, line_send, line_recv,
):
    pts, sens = lax.axis_index("pts"), lax.axis_index("sens")
    x, zh, y = pts % 4, pts // 4 % 2, pts // 8
    zl, core = sens // 2, sens % 2

    def plane(dx, dy):
        tx, ty = (x + dx) % 4, (y + dy) % 4
        return ty * 4 + tx, (ty * 2 + zh) * 4 + tx

    own_chunk = y * 4 + x
    z_peer = (y * 2 + 1 - zh) * 4 + x
    up, down = (pts + 1) % 32, (pts + 31) % 32
    core_peer = zl * 2 + 1 - core
    line = [3 - zl, (zl + 2) % 4, zl + 1 - 2 * (zl % 2), zl]

    loads = [
        pltpu.make_async_copy(src, dst, load_sem.at[i])
        for i, (src, dst) in enumerate(
            [
                (kern_hbm, kern), (fh_hbm, fh), (fl_hbm, fl), (vec_hbm, vec), (corr_hbm, corr),
                (stiff_hbm, stiff), (coup_hbm, coup), (nbr_hbm, nbr),
            ]
        )
    ]
    for copy in loads:
        copy.start()

    barrier = pltpu.get_barrier_semaphore()
    greet = [{"pts": plane(dx, dy)[1]} for dx, dy in PLANE]
    greet += [{"pts": z_peer}, {"pts": up}, {"pts": down}, {"sens": core_peer}]
    greet += [{"sens": line[i] * 2 + core} for i in range(3)]
    for target in greet:
        pl.semaphore_signal(barrier, inc=1, device_id=target, device_id_type=pl.DeviceIdType.MESH)

    def remote(src, dst, send, recv, target):
        return pltpu.make_async_remote_copy(
            src_ref=src, dst_ref=dst, send_sem=send, recv_sem=recv,
            device_id=target, device_id_type=pl.DeviceIdType.MESH,
        )

    freq = lax.broadcasted_iota(jnp.int32, (1, F2), 1)
    weight = jnp.where(freq % NT == 0, 1.0 / F2, 2.0 / F2).astype(F32)

    for i in range(3):
        loads[i].wait()
    forward = jnp.concatenate([fh[...], fh[...], fl[...]], axis=0)

    @pl.loop(0, 2)
    def _(i):
        rows = kern[pl.ds(i * 4, 4)].reshape(4 * PD, NT)
        hat = matmul(stack(rows), forward) * weight
        kh[pl.ds(i * 4, 4)] = hat.reshape(4, PD, F2)
        km[pl.ds(i * 4, 4)] = (hat[:, :NT] - hat[:, NT:]).reshape(4, PD, NT)

    loads[3].wait()

    @pl.loop(0, 2)
    def _(i):
        rows = vec[pl.ds(i * 4, 4)].reshape(4 * PD, NT)
        vh[pl.ds(i * 4, 4)] = matmul(stack(rows), forward).reshape(4, PD, F2)

    lane = lax.broadcasted_iota(jnp.int32, (8, LANES), 1)

    @pl.loop(0, FT * (SD // 2))
    def _(it):
        ft, s0 = it // (SD // 2), it % (SD // 2) * 2
        re = pl.ds(pl.multiple_of(ft * LANES, LANES), LANES)
        im = pl.ds(pl.multiple_of(NT + ft * LANES, LANES), LANES)
        keep = lane + ft * LANES > 0
        acc = [[None] * K for _ in range(6)]
        for p in range(PD // 8):
            rows = pl.ds(p * 8, 8)
            right = []
            for j in range(2):
                c, d = kh[s0 + j, rows, re], kh[s0 + j, rows, im]
                right.append((c, d, c + d))
            for k in range(K):
                a, b = vh[k, rows, re], vh[k, rows, im]
                left = (a, b, a + b)
                for j in range(2):
                    for q in range(3):
                        term = left[q] * right[j][q]
                        old = acc[j * 3 + q][k]
                        acc[j * 3 + q][k] = term if old is None else old + term
        for j in range(2):
            p1, p2, p3 = (
                jnp.concatenate([jnp.sum(v, axis=0, keepdims=True) for v in acc[j * 3 + q]], axis=0)
                for q in range(3)
            )
            rows = pl.ds(pl.multiple_of((s0 + j) * 8, 8), 8)
            ph[rows, re] = jnp.where(keep, p1 - p2, p1)
            ph[rows, im] = jnp.where(keep, p3 - p1 - p2, p2)

    inverse = jnp.concatenate([fh[...], fh[...], fl[...]], axis=1)
    pred = matmul_t(stack(ph[...]), inverse)
    for c in range(16):
        part[c] = pred[c * 4 : c * 4 + 4]

    pl.semaphore_wait(barrier, len(greet))

    rs = []
    for i, (dx, dy) in enumerate(PLANE):
        chunk, target = plane(dx, dy)
        rs.append(remote(part.at[chunk], rs_in.at[i], rs_send.at[i], rs_recv.at[i], {"pts": target}))
        rs[-1].start()
    halo = [
        remote(vec.at[sens, pl.ds(PD - COLS, COLS)], halo_lo, halo_send.at[0], halo_recv.at[0], {"pts": up}),
        remote(vec.at[sens, pl.ds(0, COLS)], halo_hi, halo_send.at[1], halo_recv.at[1], {"pts": down}),
    ]
    for copy in halo:
        copy.start()

    loads[4].wait()
    sensor = own_chunk // 2
    scale = noise[sensor]
    mix_high, mix_low = split(corr[group[sensor]])
    mix = jnp.concatenate([mix_high, mix_high, mix_low], axis=1)

    total = part[own_chunk]
    for i in range(len(PLANE) - 1, -1, -1):
        rs[i].wait_recv()
        total = total + rs_in[i]
    zsum[...] = total
    swap = remote(zsum, z_in, z_send, z_recv, {"pts": z_peer})
    swap.start()

    for i in range(5, 8):
        loads[i].wait()
    for copy in halo:
        copy.wait_recv()
    q = lax.broadcasted_iota(jnp.int32, (PD + 2 * COLS, PD), 0)
    here = lax.broadcasted_iota(jnp.int32, (PD + 2 * COLS, PD), 1) + COLS
    local = nbr[...] - pts * PD + COLS
    links = coup[...]
    diagonal = stiff[...] + jnp.sum(links, axis=0, keepdims=True)
    pick = jnp.where(q == here, diagonal, 0.0)
    for j in range(4):
        pick = pick - jnp.where(q == local[j : j + 1], links[j : j + 1], 0.0)
    padded = jnp.concatenate([halo_lo[...], vec[sens], halo_hi[...]], axis=0)
    prior[...] = lax.dot_general(
        pick, padded, (((0,), (0,)), ((), ())),
        precision=lax.Precision.HIGHEST, preferred_element_type=F32,
    )

    swap.wait_recv()
    total = zsum[...] + z_in[...]
    tall = jnp.concatenate([total, jnp.zeros((12, NT), F32)], axis=0)
    mixed = matmul_t(stack(tall), mix)[:4]
    value = scale * (total + mixed)
    mine[...] = value
    resid[own_chunk] = value
    ag = []
    for i, (dx, dy) in enumerate(PLANE):
        _, target = plane(dx, dy)
        ag.append(remote(mine, resid.at[own_chunk], ag_send.at[i], ag_recv.at[i], {"pts": target}))
        ag[-1].start()
    for i, (dx, dy) in enumerate(PLANE):
        source = plane(-dx, -dy)[0]
        remote(mine, resid.at[source], ag_send.at[i], ag_recv.at[i], {"pts": up}).wait_recv()

    rows = jnp.concatenate([resid[c] for c in range(16)], axis=0)
    hat = matmul(stack(rows), forward)
    for c in range(2 * FT):
        rh[c] = hat[:, c * LANES : (c + 1) * LANES]

    core_copies, line_copies = [], []
    for i in range(4):
        first = line[i] * 2 + 1 - core
        second = line[i] * 2 + core

        @pl.loop(0, 2 * FT)
        def _(it, first=first, second=second):
            ft, which = it // 2, it % 2
            k = first + which * (second - first)
            re = pl.ds(pl.multiple_of(ft * LANES, LANES), LANES)
            im = pl.ds(pl.multiple_of(NT + ft * LANES, LANES), LANES)
            keep = lane + ft * LANES > 0
            left = []
            for s in range(SD):
                a = rh[ft, pl.ds(s * 8 + k, 8, stride=0), :]
                b = rh[FT + ft, pl.ds(s * 8 + k, 8, stride=0), :]
                left.append((a, b, a + b))
            for p in range(PD // 8):
                rows = pl.ds(p * 8, 8)
                p1 = p2 = p3 = None
                for s in range(SD):
                    t1 = left[s][0] * kh[s, rows, re]
                    t2 = left[s][1] * kh[s, rows, im]
                    t3 = left[s][2] * km[s, rows, re]
                    p1, p2, p3 = (t1, t2, t3) if s == 0 else (p1 + t1, p2 + t2, p3 + t3)
                here = pl.ds(pl.multiple_of(which * PD + p * 8, 8), 8)
                grad[here, re] = jnp.where(keep, p1 + p2, p1)
                grad[here, im] = jnp.where(keep, p3 - p1 + p2, p2)

        data = matmul_t(stack(grad[...]), inverse)
        core_out[i] = data[:PD]
        copy = remote(core_out.at[i], core_in.at[i], core_send.at[i], core_recv.at[i], {"sens": core_peer})
        copy.start()
        core_copies.append(copy)
        line_out[i] = data[PD:]
        if i:
            finish(i - 1, core_copies, core_in, line_out)
            copy = remote(
                line_out.at[i - 1], line_in.at[i - 1], line_send.at[i - 1], line_recv.at[i - 1],
                {"sens": line[i - 1] * 2 + core},
            )
            copy.start()
            line_copies.append(copy)
    finish(3, core_copies, core_in, line_out)
    result = line_out[3] + prior[...]
    for i in (2, 1, 0):
        line_copies[i].wait_recv()
        result = result + line_in[i]
    out_ref[0] = result

    for copy in halo + rs + [swap] + ag + core_copies + line_copies:
        copy.wait_send()


def finish(i, core_copies, core_in, line_out):
    core_copies[i].wait_recv()
    line_out[i] = line_out[i] + core_in[i]


def local(kernel, vectors, noise_scale, sensor_group, correlation, stiffness, couplings, neighbors):
    high, low = table()
    anywhere = pl.BlockSpec(memory_space=pl.ANY)
    smem = pl.BlockSpec(memory_space=pltpu.SMEM)
    dma = pltpu.SemaphoreType.DMA
    count = len(PLANE)
    return pl.pallas_call(
        body,
        out_shape=jax.ShapeDtypeStruct((1, PD, NT), F32),
        in_specs=[anywhere, anywhere, smem, smem] + [anywhere] * 6,
        out_specs=pl.BlockSpec(memory_space=pltpu.VMEM),
        scratch_shapes=[
            pltpu.VMEM((SD, PD, NT), F32),
            pltpu.VMEM((K, PD, NT), F32),
            pltpu.VMEM((NB, NT, NT), F32),
            pltpu.VMEM((1, PD), F32),
            pltpu.VMEM((4, PD), F32),
            pltpu.VMEM((4, PD), jnp.int32),
            pltpu.VMEM((NT, F2), BF16),
            pltpu.VMEM((NT, F2), BF16),
            pltpu.VMEM((SD, PD, F2), F32),
            pltpu.VMEM((SD, PD, NT), F32),
            pltpu.VMEM((K, PD, F2), F32),
            pltpu.VMEM((SD * K, F2), F32),
            pltpu.VMEM((16, 4, NT), F32),
            pltpu.VMEM((count, 4, NT), F32),
            pltpu.VMEM((4, NT), F32),
            pltpu.VMEM((4, NT), F32),
            pltpu.VMEM((4, NT), F32),
            pltpu.VMEM((16, 4, NT), F32),
            pltpu.VMEM((2 * FT, SD * K, LANES), F32),
            pltpu.VMEM((2 * PD, F2), F32),
            pltpu.VMEM((PD, NT), F32),
            pltpu.VMEM((COLS, NT), F32),
            pltpu.VMEM((COLS, NT), F32),
            pltpu.VMEM((4, PD, NT), F32),
            pltpu.VMEM((4, PD, NT), F32),
            pltpu.VMEM((4, PD, NT), F32),
            pltpu.VMEM((3, PD, NT), F32),
            dma((8,)),
            dma((2,)), dma((2,)),
            dma((count,)), dma((count,)),
            dma, dma,
            dma((count,)), dma((count,)),
            dma((4,)), dma((4,)),
            dma((3,)), dma((3,)),
        ],
        compiler_params=pltpu.CompilerParams(collective_id=0, has_side_effects=True),
    )(
        kernel, vectors, noise_scale, sensor_group, correlation, stiffness.reshape(1, PD),
        couplings, neighbors, jnp.asarray(high), jnp.asarray(low),
    )


def solution(mesh):
    in_specs = (
        P("sens", "pts", None),
        P(None, "pts", None),
        P("sens"),
        P("sens"),
        P(),
        P("pts"),
        P(None, "pts"),
        P(None, "pts"),
    )
    return jax.shard_map(
        local, mesh=mesh, in_specs=in_specs, out_specs=P("sens", "pts", None), check_vma=False
    )
```

time: 541 us -> 45.9 us (0.08)
  waiting for transfers between devices: 413 us -> 0 us
  matrix products: 60.8 us -> 0 us
  Pallas kernels: 0 us -> 44.2 us
  local copies, waits for them, and re-layouts: 33.8 us -> 1.54 us
  between operations: 13.9 us -> 0.01 us
  other arithmetic: 10.4 us -> 0 us
    psum x1 -> x0, waiting for transfers between devices: 377 us -> none  [local(): predicted = lax.psum(flat, 'pts')]
    dot_general x17 -> x0, matrix products: 60.8 us -> none  [the longest x2 11.2 us: spectral(): prod_yy = jnp.einsum(form, left_y, right_y, precision=HIGHEST)]
    pallas_call x0 -> x1, Pallas kernels: none -> 44.2 us  [local(): pl.pallas_call(body, out_shape=jax.ShapeDtypeStruct((1, PD, NT), F32), in...]
    reduce_scatter x1 -> x0, waiting for transfers between devices: 35.2 us -> none  [local(): lax.psum_scatter(jnp.einsum('kpf,ft->kpt', grad_hat, inverse, precision=H...]
    slice x12 -> x0, local copies, waits for them, and re-layouts: 24.1 us -> none  [the longest x5 13 us: spectral(): right_x, right_y = (right[..., :half], right[..., half:])]
  transfers between devices with their start and end apart: 4 -> 0, of which waited for: 3 -> 0; matrix products, arithmetic and copies ran while one was open for 2% -> 0% of each run, Pallas kernels for 0% -> 0%
where the time goes in v1:
time: 45.9 us; the launch traced here: 45.7 us
  Pallas kernels  44.2 us (96%)
  local copies, waits for them, and re-layouts  1.54 us (3%)
    pallas_call x1, Pallas kernels, local(): pl.pallas_call(body, out_shape=jax.ShapeDtypeStruct((1, PD, NT), F32), in...  44.2 us
    unnamed x1, local copies, waits for them, and re-layouts  1.54 us

profile of v1, /device:TPU:1, one launch (start us, length us, event | category | flops | bytes accessed | tf_op | source)
XLA Modules:
  0.0 45.7 jit_solution(11757823784485443117)
XLA Ops:
  0.0 44.2 %shard_map.100 = f32[1,64,384]{2,1,0:T(8,128)} custom-call(f32[8,64,384]{2,1,0:T(8,128)} %kern_hbm.1, f32[8,64,384]{2,1,0:T(8,128)} %vec_hbm.1, f32[8]{0:T(128)} %noise.1, s32[8]{0:T(128)} %group.1, f32[4,384,384]{2,1,0:T(8,128)} %corr_hbm.1, f32[1,64]{1,0:T(1,128)} %bitcast.1, f32[4,64]{1,0:T(4,128)} %coup_hbm.1, s32[4,64]{1,0:T(4,128)} %nbr_hbm.1, ...), custom_call_target="tpu_custom_call" | custom-call | tf_op jit(solution)/shard_map/pallas_call | solution.py:291
  44.2 1.5 %copy.12 = f32[1,64,384]{2,1,0:T(8,128)} copy(f32[1,64,384]{2,1,0:T(8,128)} %shard_map.100) | data formatting | bytes 196608

commit v2 on v1

v2 whole, which is shorter than its diff:
```python
import contextlib
import math

import jax
import jax.numpy as jnp
import numpy as np
from jax import lax
from jax.experimental import pallas as pl
from jax.experimental.pallas import tpu as pltpu
from jax.sharding import PartitionSpec as P

F32, BF16 = jnp.float32, jnp.bfloat16
phase = lambda name: contextlib.nullcontext()
K, NT, NB, SD, PD, COLS = 8, 384, 4, 8, 64, 16
F2 = 2 * NT
LANES = 128
FT = NT // LANES
VECTORS = (0, 2, 4, 6, 1, 3, 5, 7)
SUB = 2
PLANE = sorted(
    ((dx, dy) for dx in range(4) for dy in range(4) if dx or dy),
    key=lambda d: -(min(d[0], 4 - d[0]) + min(d[1], 4 - d[1])),
)


def table():
    t = np.arange(NT)
    angle = 2.0 * math.pi / F2 * (t[:, None] * t[None, :] % F2)
    second = -np.sin(angle)
    second[:, 0] = np.where(t % 2 == 0, 1.0, -1.0)
    full = np.concatenate([np.cos(angle), second], axis=1).astype(np.float32)
    high = full.astype(BF16)
    low = (full - high.astype(np.float32)).astype(BF16)
    return high, low


def split(x):
    high = x.astype(BF16)
    low = (x - high.astype(F32)).astype(BF16)
    return high, low


def stack(x):
    high, low = split(x)
    return jnp.concatenate([high, low, high], axis=1)


def matmul(a, b):
    return lax.dot_general(a, b, (((1,), (0,)), ((), ())), preferred_element_type=F32)


def matmul_t(a, b):
    return lax.dot_general(a, b, (((1,), (1,)), ((), ())), preferred_element_type=F32)


def body(
    kern_hbm, vec_hbm, noise, group, corr_hbm, stiff_hbm, coup_hbm, nbr_hbm, fh_hbm, fl_hbm,
    out_ref,
    kern, vec, corr, stiff, coup, nbr, fh, fl,
    kh, km, vh, ph, part, rs_in, zsum, z_in, mine, resid, rh, grad, prior,
    halo_lo, halo_hi, line_out, line_in,
    load_sem, halo_send, halo_recv, rs_send, rs_recv, z_send, z_recv, ag_send, ag_recv,
    share_send, share_recv, line_send, line_recv,
):
    pts, sens = lax.axis_index("pts"), lax.axis_index("sens")
    x, zh, y = pts % 4, pts // 4 % 2, pts // 8
    zl, core = sens // 2, sens % 2

    def plane(dx, dy):
        tx, ty = (x + dx) % 4, (y + dy) % 4
        return ty * 4 + tx, (ty * 2 + zh) * 4 + tx

    own_chunk = y * 4 + x
    z_peer = (y * 2 + 1 - zh) * 4 + x
    up, down = (pts + 1) % 32, (pts + 31) % 32
    core_peer = zl * 2 + 1 - core
    half = x % 2
    order = [3 - zl, (12 - 2 * zl) % 5, 3 - (12 - 2 * zl) % 5, zl]
    heads = [1 + zl % 2, order[1], order[2]]
    inner = zl * (3 - zl) // 2

    loads = [
        pltpu.make_async_copy(src, dst, load_sem.at[i])
        for i, (src, dst) in enumerate(
            [
                (kern_hbm, kern), (fh_hbm, fh), (fl_hbm, fl), (vec_hbm, vec), (corr_hbm, corr),
                (stiff_hbm, stiff), (coup_hbm, coup), (nbr_hbm, nbr),
            ]
        )
    ]
    for copy in loads:
        copy.start()

    barrier = pltpu.get_barrier_semaphore()
    greet = [{"pts": plane(dx, dy)[1]} for dx, dy in PLANE]
    greet += [{"pts": plane(dx, dy)[1], "sens": core_peer} for dx, dy in PLANE]
    greet += [{"pts": z_peer}, {"pts": up}, {"pts": down}, {"sens": core_peer}]
    greet += [{"sens": (zl + i) % 4 * 2 + core} for i in range(1, 4)]
    for target in greet:
        pl.semaphore_signal(barrier, inc=1, device_id=target, device_id_type=pl.DeviceIdType.MESH)

    def remote(src, dst, send, recv, target):
        return pltpu.make_async_remote_copy(
            src_ref=src, dst_ref=dst, send_sem=send, recv_sem=recv,
            device_id=target, device_id_type=pl.DeviceIdType.MESH,
        )

    freq = lax.broadcasted_iota(jnp.int32, (1, F2), 1)
    weight = jnp.where(freq % NT == 0, 1.0 / F2, 2.0 / F2).astype(F32)

    with phase("p_load"):
        for i in range(3):
            loads[i].wait()
    forward = jnp.concatenate([fh[...], fh[...], fl[...]], axis=0)

    with phase("p_kdft"):
        @pl.loop(0, 2)
        def _(i):
            rows = kern[pl.ds(i * 4, 4)].reshape(4 * PD, NT)
            hat = matmul(stack(rows), forward) * weight
            kh[pl.ds(i * 4, 4)] = hat.reshape(4, PD, F2)
            km[pl.ds(i * 4, 4)] = (hat[:, :NT] - hat[:, NT:]).reshape(4, PD, NT)

    loads[3].wait()

    with phase("p_vdft"):
        @pl.loop(0, 2)
        def _(i):
            rows = vec[pl.ds(i * 4, 4)].reshape(4 * PD, NT)
            vh[pl.ds(i * 4, 4)] = matmul(stack(rows), forward).reshape(4, PD, F2)

    lane = lax.broadcasted_iota(jnp.int32, (8, LANES), 1)

    with phase("p_spec"):
        @pl.loop(0, FT * (SD // 2))
        def _(it):
            ft, s0 = it // (SD // 2), it % (SD // 2) * 2
            re = pl.ds(pl.multiple_of(ft * LANES, LANES), LANES)
            im = pl.ds(pl.multiple_of(NT + ft * LANES, LANES), LANES)
            keep = lane + ft * LANES > 0
            acc = [[None] * K for _ in range(6)]
            for p in range(PD // 8):
                rows = pl.ds(p * 8, 8)
                right = []
                for j in range(2):
                    c, d = kh[s0 + j, rows, re], kh[s0 + j, rows, im]
                    right.append((c, d, c + d))
                for k in range(K):
                    a, b = vh[VECTORS[k], rows, re], vh[VECTORS[k], rows, im]
                    left = (a, b, a + b)
                    for j in range(2):
                        for q in range(3):
                            term = left[q] * right[j][q]
                            old = acc[j * 3 + q][k]
                            acc[j * 3 + q][k] = term if old is None else old + term
            for j in range(2):
                p1, p2, p3 = (
                    jnp.concatenate([jnp.sum(v, axis=0, keepdims=True) for v in acc[j * 3 + q]], axis=0)
                    for q in range(3)
                )
                rows = pl.ds(pl.multiple_of((s0 + j) * 8, 8), 8)
                ph[rows, re] = jnp.where(keep, p1 - p2, p1)
                ph[rows, im] = jnp.where(keep, p3 - p1 - p2, p2)

    inverse = jnp.concatenate([fh[...], fh[...], fl[...]], axis=1)
    with phase("p_inv"):
        pred = matmul_t(stack(ph[...]), inverse)
        for c in range(16):
            part[c] = pred[c * 4 : c * 4 + 4]

    with phase("p_bar"):
        pl.semaphore_wait(barrier, len(greet))

    rs = []
    for i, (dx, dy) in enumerate(PLANE):
        chunk, target = plane(dx, dy)
        rs.append(remote(part.at[chunk], rs_in.at[i], rs_send.at[i], rs_recv.at[i], {"pts": target}))
        rs[-1].start()
    halo = [
        remote(vec.at[sens, pl.ds(PD - COLS, COLS)], halo_lo, halo_send.at[0], halo_recv.at[0], {"pts": up}),
        remote(vec.at[sens, pl.ds(0, COLS)], halo_hi, halo_send.at[1], halo_recv.at[1], {"pts": down}),
    ]
    share = remote(kh.at[pl.ds(0, SD)], kh.at[pl.ds(SD, SD)], share_send, share_recv, {"sens": core_peer})
    for copy in halo + [share]:
        copy.start()

    loads[4].wait()
    sensor = own_chunk // 2
    scale = noise[sensor]
    mix_high, mix_low = split(corr[group[sensor]])
    mix = jnp.concatenate([mix_high, mix_high, mix_low], axis=1)

    with phase("p_prior"):
        for i in range(5, 8):
            loads[i].wait()
        for copy in halo:
            copy.wait_recv()
        q = lax.broadcasted_iota(jnp.int32, (PD + 2 * COLS, PD), 0)
        here = lax.broadcasted_iota(jnp.int32, (PD + 2 * COLS, PD), 1) + COLS
        local = nbr[...] - pts * PD + COLS
        links = coup[...]
        diagonal = stiff[...] + jnp.sum(links, axis=0, keepdims=True)
        pick = jnp.where(q == here, diagonal, 0.0)
        for j in range(4):
            pick = pick - jnp.where(q == local[j : j + 1], links[j : j + 1], 0.0)
        padded = jnp.concatenate([halo_lo[...], vec[sens], halo_hi[...]], axis=0)
        prior[...] = lax.dot_general(
            pick, padded, (((0,), (0,)), ((), ())),
            precision=lax.Precision.HIGHEST, preferred_element_type=F32,
        )

    total = part[own_chunk]
    with phase("p_rswait"):
        for i in range(len(PLANE) - 1, -1, -1):
            rs[i].wait_recv()
            total = total + rs_in[i]
    zsum[...] = total
    swap = remote(zsum, z_in, z_send, z_recv, {"pts": z_peer})
    swap.start()

    with phase("p_zwait"):
        swap.wait_recv()
    total = zsum[...] + z_in[...]
    tall = jnp.concatenate([total, jnp.zeros((12, NT), F32)], axis=0)
    mixed = matmul_t(stack(tall), mix)[:4]
    value = scale * (total + mixed)
    mine[...] = value
    slot = sensor + SD * ((half + core) % 2)
    home = resid.at[slot]
    ag = []
    for i, (dx, dy) in enumerate(PLANE):
        target = {"pts": plane(dx, dy)[1], "sens": zl * 2 + half}
        ag.append(remote(mine, home, ag_send.at[i], ag_recv.at[slot], target))
        ag[-1].start()
    beside = remote(mine, home, ag_send.at[len(PLANE)], ag_recv.at[slot], {"sens": core_peer})

    @pl.when(half == core)
    def _():
        resid[slot] = value

    @pl.when(half != core)
    def _():
        beside.start()

    with phase("p_share"):
        share.wait_recv()
        for s in range(SD, 2 * SD):
            km[s] = kh[s, :, :NT] - kh[s, :, NT:]

    with phase("p_agwait"):
        for i in range(2 * SD):

            @pl.when((half + core) % 2 * 2 * SD + (slot - i) * (slot - i) > 0)
            def _(i=i):
                remote(mine, resid.at[i], ag_send.at[0], ag_recv.at[i], {"sens": core_peer}).wait_recv()

    with phase("p_rdft"):
        rows = jnp.concatenate([resid[c] for c in range(2 * SD)], axis=0)
        hat = matmul(stack(rows), forward)
        for c in range(2 * FT):
            rh[c] = hat[:, c * LANES : (c + 1) * LANES]

    rows_sub = PD // SUB

    def line_copy(i, j):
        piece = pl.ds(j * rows_sub, rows_sub)
        seat = 3 * (1 - inner) if i == 0 else i
        return remote(
            line_out.at[i, piece], line_in.at[seat, piece], line_send.at[i, j], line_recv.at[seat, j],
            {"sens": heads[i] * 2 + core},
        )

    def line_arrival(i, j):
        piece = pl.ds(j * rows_sub, rows_sub)
        return remote(
            line_out.at[0, piece], line_in.at[i, piece], line_send.at[0, j], line_recv.at[i, j],
            {"sens": core_peer},
        )

    for i in range(4):
        v = order[i]

        with phase("p_adj%d" % i):

            @pl.loop(0, FT)
            def _(ft, v=v):
                re = pl.ds(pl.multiple_of(ft * LANES, LANES), LANES)
                im = pl.ds(pl.multiple_of(NT + ft * LANES, LANES), LANES)
                keep = lane + ft * LANES > 0
                acc = [None] * (PD // 8)
                for s in range(2 * SD):
                    a = rh[ft, pl.ds(s * 4 + v, 8, stride=0), :]
                    b = rh[FT + ft, pl.ds(s * 4 + v, 8, stride=0), :]
                    ab = a + b
                    for p in range(PD // 8):
                        rows = pl.ds(p * 8, 8)
                        terms = (a * kh[s, rows, re], b * kh[s, rows, im], ab * km[s, rows, re])
                        acc[p] = terms if s == 0 else tuple(m + n for m, n in zip(acc[p], terms, strict=True))
                for p in range(PD // 8):
                    p1, p2, p3 = acc[p]
                    grad[pl.ds(p * 8, 8), re] = jnp.where(keep, p1 + p2, p1)
                    grad[pl.ds(p * 8, 8), im] = jnp.where(keep, p3 - p1 + p2, p2)

        with phase("p_ainv%d" % i):
            line_out[i] = matmul_t(stack(grad[...]), inverse)
        if i < 2:
            for j in range(SUB):
                line_copy(i, j).start()
        if i == 2:

            @pl.when(inner == 0)
            def _():
                for j in range(SUB):
                    line_copy(2, j).start()

    with phase("p_relay"):

        @pl.when(inner == 1)
        def _():
            for j in range(SUB):
                line_arrival(3, j).wait_recv()
                piece = pl.ds(j * rows_sub, rows_sub)
                line_out[2, piece] = line_out[2, piece] + line_in[3, piece]
                line_copy(2, j).start()

    prior[...] = prior[...] + line_out[3]

    with phase("p_linewait"):

        @pl.when(inner == 1)
        def _():
            for j in range(SUB):
                line_arrival(0, j).wait_recv()
            prior[...] = prior[...] + line_in[0]

        for i in (1, 2):
            for j in range(SUB):
                line_arrival(i, j).wait_recv()
        out_ref[0] = prior[...] + line_in[1] + line_in[2]

    with phase("p_sends"):
        for copy in halo + rs + [swap, share] + ag + [line_copy(i, j) for i in range(3) for j in range(SUB)]:
            copy.wait_send()

        @pl.when(half != core)
        def _():
            beside.wait_send()


def local(kernel, vectors, noise_scale, sensor_group, correlation, stiffness, couplings, neighbors):
    high, low = table()
    anywhere = pl.BlockSpec(memory_space=pl.ANY)
    smem = pl.BlockSpec(memory_space=pltpu.SMEM)
    dma = pltpu.SemaphoreType.DMA
    count = len(PLANE)
    return pl.pallas_call(
        body,
        out_shape=jax.ShapeDtypeStruct((1, PD, NT), F32),
        in_specs=[anywhere, anywhere, smem, smem] + [anywhere] * 6,
        out_specs=pl.BlockSpec(memory_space=pltpu.VMEM),
        scratch_shapes=[
            pltpu.VMEM((SD, PD, NT), F32),
            pltpu.VMEM((K, PD, NT), F32),
            pltpu.VMEM((NB, NT, NT), F32),
            pltpu.VMEM((1, PD), F32),
            pltpu.VMEM((4, PD), F32),
            pltpu.VMEM((4, PD), jnp.int32),
            pltpu.VMEM((NT, F2), BF16),
            pltpu.VMEM((NT, F2), BF16),
            pltpu.VMEM((2 * SD, PD, F2), F32),
            pltpu.VMEM((2 * SD, PD, NT), F32),
            pltpu.VMEM((K, PD, F2), F32),
            pltpu.VMEM((SD * K, F2), F32),
            pltpu.VMEM((16, 4, NT), F32),
            pltpu.VMEM((count, 4, NT), F32),
            pltpu.VMEM((4, NT), F32),
            pltpu.VMEM((4, NT), F32),
            pltpu.VMEM((4, NT), F32),
            pltpu.VMEM((16, 4, NT), F32),
            pltpu.VMEM((2 * FT, SD * K, LANES), F32),
            pltpu.VMEM((PD, F2), F32),
            pltpu.VMEM((PD, NT), F32),
            pltpu.VMEM((COLS, NT), F32),
            pltpu.VMEM((COLS, NT), F32),
            pltpu.VMEM((4, PD, NT), F32),
            pltpu.VMEM((4, PD, NT), F32),
            dma((8,)),
            dma((2,)), dma((2,)),
            dma((count,)), dma((count,)),
            dma, dma,
            dma((count + 1,)), dma((2 * SD,)),
            dma, dma,
            dma((3, SUB)), dma((4, SUB)),
        ],
        compiler_params=pltpu.CompilerParams(collective_id=0, has_side_effects=True),
    )(
        kernel, vectors, noise_scale, sensor_group, correlation, stiffness.reshape(1, PD),
        couplings, neighbors, jnp.asarray(high), jnp.asarray(low),
    )


def solution(mesh):
    in_specs = (
        P("sens", "pts", None),
        P(None, "pts", None),
        P("sens"),
        P("sens"),
        P(),
        P("pts"),
        P(None, "pts"),
        P(None, "pts"),
    )
    return jax.shard_map(
        local, mesh=mesh, in_specs=in_specs, out_specs=P("sens", "pts", None), check_vma=False
    )
```

time: 45.9 us -> 44 us (0.959)
  Pallas kernels: 44.2 us -> 42.3 us
    pallas_call x1, Pallas kernels: 44.2 us -> 42.3 us  [local(): pl.pallas_call(body, out_shape=jax.ShapeDtypeStruct((1, PD, NT), F32), in...]
where the time goes in v2:
time: 44 us; the launch traced here: 43.9 us
  Pallas kernels  42.3 us (96%)
  local copies, waits for them, and re-layouts  1.54 us (4%)
    pallas_call x1, Pallas kernels, local(): pl.pallas_call(body, out_shape=jax.ShapeDtypeStruct((1, PD, NT), F32), in...  42.3 us
    unnamed x1, local copies, waits for them, and re-layouts  1.54 us

profile of v2, /device:TPU:1, one launch (start us, length us, event | category | flops | bytes accessed | tf_op | source)
XLA Modules:
  0.0 43.9 jit_solution(4384342284670284027)
XLA Ops:
  0.0 42.3 %shard_map.100 = f32[1,64,384]{2,1,0:T(8,128)} custom-call(f32[8,64,384]{2,1,0:T(8,128)} %kern_hbm.1, f32[8,64,384]{2,1,0:T(8,128)} %vec_hbm.1, f32[8]{0:T(128)} %noise.1, s32[8]{0:T(128)} %group.1, f32[4,384,384]{2,1,0:T(8,128)} %corr_hbm.1, f32[1,64]{1,0:T(1,128)} %bitcast.1, f32[4,64]{1,0:T(4,128)} %coup_hbm.1, s32[4,64]{1,0:T(4,128)} %nbr_hbm.1, ...), custom_call_target="tpu_custom_call" | custom-call | tf_op jit(solution)/shard_map/pallas_call | solution.py:356
  42.3 1.5 %copy.12 = f32[1,64,384]{2,1,0:T(8,128)} copy(f32[1,64,384]{2,1,0:T(8,128)} %shard_map.100) | data formatting | bytes 196608

commit v3 on v2

--- a/solution.py
+++ b/solution.py
@@ -28,7 +28,8 @@
     angle = 2.0 * math.pi / F2 * (t[:, None] * t[None, :] % F2)
     second = -np.sin(angle)
     second[:, 0] = np.where(t % 2 == 0, 1.0, -1.0)
-    full = np.concatenate([np.cos(angle), second], axis=1).astype(np.float32)
+    parts = [np.cos(angle).reshape(NT, FT, 1, LANES), second.reshape(NT, FT, 1, LANES)]
+    full = np.concatenate(parts, axis=2).reshape(NT, F2).astype(np.float32)
     high = full.astype(BF16)
     low = (full - high.astype(np.float32)).astype(BF16)
     return high, low
@@ -54,10 +55,10 @@
 
 
 def body(
-    kern_hbm, vec_hbm, noise, group, corr_hbm, stiff_hbm, coup_hbm, nbr_hbm, fh_hbm, fl_hbm,
+    kern_hbm, vec_hbm, noise_hbm, group_hbm, corr_hbm, stiff_hbm, coup_hbm, nbr_hbm, fh_hbm, fl_hbm,
     out_ref,
-    kern, vec, corr, stiff, coup, nbr, fh, fl,
-    kh, km, vh, ph, part, rs_in, zsum, z_in, mine, resid, rh, grad, prior,
+    kern, vec, corr, stiff, coup, nbr, fh, fl, noise, group, lhs,
+    kh, km, vh, ph, part, rs_in, zsum, z_in, mine, resid, rh, grad_a, grad_b, prior,
     halo_lo, halo_hi, line_out, line_in,
     load_sem, halo_send, halo_recv, rs_send, rs_recv, z_send, z_recv, ag_send, ag_recv,
     share_send, share_recv, line_send, line_recv,
@@ -74,6 +75,7 @@
     z_peer = (y * 2 + 1 - zh) * 4 + x
     up, down = (pts + 1) % 32, (pts + 31) % 32
     core_peer = zl * 2 + 1 - core
+    grads = (grad_a, grad_b)
     half = x % 2
     order = [3 - zl, (12 - 2 * zl) % 5, 3 - (12 - 2 * zl) % 5, zl]
     heads = [1 + zl % 2, order[1], order[2]]
@@ -84,7 +86,7 @@
         for i, (src, dst) in enumerate(
             [
                 (kern_hbm, kern), (fh_hbm, fh), (fl_hbm, fl), (vec_hbm, vec), (corr_hbm, corr),
-                (stiff_hbm, stiff), (coup_hbm, coup), (nbr_hbm, nbr),
+                (stiff_hbm, stiff), (coup_hbm, coup), (nbr_hbm, nbr), (noise_hbm, noise), (group_hbm, group),
             ]
         )
     ]
@@ -106,38 +108,32 @@
         )
 
     freq = lax.broadcasted_iota(jnp.int32, (1, F2), 1)
-    weight = jnp.where(freq % NT == 0, 1.0 / F2, 2.0 / F2).astype(F32)
-
-    with phase("p_load"):
-        for i in range(3):
-            loads[i].wait()
-    forward = jnp.concatenate([fh[...], fh[...], fl[...]], axis=0)
-
-    with phase("p_kdft"):
-        @pl.loop(0, 2)
-        def _(i):
-            rows = kern[pl.ds(i * 4, 4)].reshape(4 * PD, NT)
-            hat = matmul(stack(rows), forward) * weight
-            kh[pl.ds(i * 4, 4)] = hat.reshape(4, PD, F2)
-            km[pl.ds(i * 4, 4)] = (hat[:, :NT] - hat[:, NT:]).reshape(4, PD, NT)
-
-    loads[3].wait()
-
-    with phase("p_vdft"):
-        @pl.loop(0, 2)
-        def _(i):
-            rows = vec[pl.ds(i * 4, 4)].reshape(4 * PD, NT)
-            vh[pl.ds(i * 4, 4)] = matmul(stack(rows), forward).reshape(4, PD, F2)
+    weight = jnp.where(freq * (freq - LANES) == 0, 1.0 / F2, 2.0 / F2).astype(F32)
 
     lane = lax.broadcasted_iota(jnp.int32, (8, LANES), 1)
 
-    with phase("p_spec"):
-        @pl.loop(0, FT * (SD // 2))
-        def _(it):
-            ft, s0 = it // (SD // 2), it % (SD // 2) * 2
-            re = pl.ds(pl.multiple_of(ft * LANES, LANES), LANES)
-            im = pl.ds(pl.multiple_of(NT + ft * LANES, LANES), LANES)
-            keep = lane + ft * LANES > 0
+    def columns(ft):
+        return slice(ft * 2 * LANES, (ft + 1) * 2 * LANES)
+
+    def parts(ft):
+        return slice(ft * 2 * LANES, ft * 2 * LANES + LANES), slice(ft * 2 * LANES + LANES, (ft + 1) * 2 * LANES)
+
+    def keep(ft, v, other):
+        return jnp.where(lane > 0, v, other) if ft == 0 else v
+
+    def transform(which, ft):
+        a = jnp.concatenate([lhs[which], lhs[which, :, :NT]], axis=1)
+        return matmul(a, jnp.concatenate([fh[:, columns(ft)], fh[:, columns(ft)], fl[:, columns(ft)]], axis=0))
+
+    def hats(ft):
+        hat = transform(0, ft) * weight[:, columns(ft)]
+        kh[0:SD, :, columns(ft)] = hat.reshape(SD, PD, 2 * LANES)
+        km[0:SD, :, ft * LANES : (ft + 1) * LANES] = (hat[:, :LANES] - hat[:, LANES:]).reshape(SD, PD, LANES)
+        vh[:, :, columns(ft)] = transform(1, ft).reshape(K, PD, 2 * LANES)
+
+    def product(ft):
+        re, im = parts(ft)
+        for s0 in range(0, SD, 2):
             acc = [[None] * K for _ in range(6)]
             for p in range(PD // 8):
                 rows = pl.ds(p * 8, 8)
@@ -158,10 +154,32 @@
                     jnp.concatenate([jnp.sum(v, axis=0, keepdims=True) for v in acc[j * 3 + q]], axis=0)
                     for q in range(3)
                 )
-                rows = pl.ds(pl.multiple_of((s0 + j) * 8, 8), 8)
-                ph[rows, re] = jnp.where(keep, p1 - p2, p1)
-                ph[rows, im] = jnp.where(keep, p3 - p1 - p2, p2)
-
+                rows = pl.ds((s0 + j) * 8, 8)
+                ph[rows, re] = keep(ft, p1 - p2, p1)
+                ph[rows, im] = keep(ft, p3 - p1 - p2, p2)
+
+    with phase("p_load"):
+        loads[0].wait()
+        high, low = split(kern[...].reshape(SD * PD, NT))
+        lhs[0, :, :NT] = high
+        lhs[0, :, NT:] = low
+        loads[3].wait()
+        high, low = split(vec[...].reshape(K * PD, NT))
+        lhs[1, :, :NT] = high
+        lhs[1, :, NT:] = low
+        loads[1].wait()
+        loads[2].wait()
+    with phase("p_front0"):
+        hats(0)
+    with phase("p_front1"):
+        hats(1)
+        product(0)
+    with phase("p_front2"):
+        hats(2)
+        product(1)
+    with phase("p_front3"):
+        product(2)
+    forward = jnp.concatenate([fh[...], fh[...], fl[...]], axis=0)
     inverse = jnp.concatenate([fh[...], fh[...], fl[...]], axis=1)
     with phase("p_inv"):
         pred = matmul_t(stack(ph[...]), inverse)
@@ -184,11 +202,45 @@
     for copy in halo + [share]:
         copy.start()
 
-    loads[4].wait()
+    for i in (4, 8, 9):
+        loads[i].wait()
     sensor = own_chunk // 2
     scale = noise[sensor]
     mix_high, mix_low = split(corr[group[sensor]])
     mix = jnp.concatenate([mix_high, mix_high, mix_low], axis=1)
+
+    total = part[own_chunk]
+    with phase("p_rswait"):
+        for i in range(len(PLANE) - 1, -1, -1):
+            rs[i].wait_recv()
+            total = total + rs_in[i]
+    zsum[...] = total
+    swap = remote(zsum, z_in, z_send, z_recv, {"pts": z_peer})
+    swap.start()
+
+    with phase("p_zwait"):
+        swap.wait_recv()
+    total = zsum[...] + z_in[...]
+    tall = jnp.concatenate([total, jnp.zeros((12, NT), F32)], axis=0)
+    mixed = matmul_t(stack(tall), mix)[:4]
+    value = scale * (total + mixed)
+    mine[...] = value
+    slot = sensor + SD * ((half + core) % 2)
+    home = resid.at[slot]
+    ag = []
+    for i, (dx, dy) in enumerate(PLANE):
+        target = {"pts": plane(dx, dy)[1], "sens": zl * 2 + half}
+        ag.append(remote(mine, home, ag_send.at[i], ag_recv.at[slot], target))
+        ag[-1].start()
+    beside = remote(mine, home, ag_send.at[len(PLANE)], ag_recv.at[slot], {"sens": core_peer})
+
+    @pl.when(half == core)
+    def _():
+        resid[slot] = value
+
+    @pl.when(half != core)
+    def _():
+        beside.start()
 
     with phase("p_prior"):
         for i in range(5, 8):
@@ -209,43 +261,12 @@
             precision=lax.Precision.HIGHEST, preferred_element_type=F32,
         )
 
-    total = part[own_chunk]
-    with phase("p_rswait"):
-        for i in range(len(PLANE) - 1, -1, -1):
-            rs[i].wait_recv()
-            total = total + rs_in[i]
-    zsum[...] = total
-    swap = remote(zsum, z_in, z_send, z_recv, {"pts": z_peer})
-    swap.start()
-
-    with phase("p_zwait"):
-        swap.wait_recv()
-    total = zsum[...] + z_in[...]
-    tall = jnp.concatenate([total, jnp.zeros((12, NT), F32)], axis=0)
-    mixed = matmul_t(stack(tall), mix)[:4]
-    value = scale * (total + mixed)
-    mine[...] = value
-    slot = sensor + SD * ((half + core) % 2)
-    home = resid.at[slot]
-    ag = []
-    for i, (dx, dy) in enumerate(PLANE):
-        target = {"pts": plane(dx, dy)[1], "sens": zl * 2 + half}
-        ag.append(remote(mine, home, ag_send.at[i], ag_recv.at[slot], target))
-        ag[-1].start()
-    beside = remote(mine, home, ag_send.at[len(PLANE)], ag_recv.at[slot], {"sens": core_peer})
-
-    @pl.when(half == core)
-    def _():
-        resid[slot] = value
-
-    @pl.when(half != core)
-    def _():
-        beside.start()
-
     with phase("p_share"):
         share.wait_recv()
         for s in range(SD, 2 * SD):
-            km[s] = kh[s, :, :NT] - kh[s, :, NT:]
+            for ft in range(FT):
+                re, im = parts(ft)
+                km[s, :, ft * LANES : (ft + 1) * LANES] = kh[s, :, re] - kh[s, :, im]
 
     with phase("p_agwait"):
         for i in range(2 * SD):
@@ -277,32 +298,31 @@
             {"sens": core_peer},
         )
 
+    def adjoint(i):
+        v, into = order[i], grads[i % 2]
+        for ft in range(FT):
+            re, im = parts(ft)
+            acc = [None] * (PD // 8)
+            for s in range(2 * SD):
+                a = rh[2 * ft, pl.ds(s * 4 + v, 8, stride=0), :]
+                b = rh[2 * ft + 1, pl.ds(s * 4 + v, 8, stride=0), :]
+                ab = a + b
+                for p in range(PD // 8):
+                    rows = pl.ds(p * 8, 8)
+                    terms = (a * kh[s, rows, re], b * kh[s, rows, im], ab * km[s, rows, ft * LANES : (ft + 1) * LANES])
+                    acc[p] = terms if s == 0 else tuple(m + n for m, n in zip(acc[p], terms, strict=True))
+            for p in range(PD // 8):
+                p1, p2, p3 = acc[p]
+                into[pl.ds(p * 8, 8), re] = keep(ft, p1 + p2, p1)
+                into[pl.ds(p * 8, 8), im] = keep(ft, p3 - p1 + p2, p2)
+
+    with phase("p_adj"):
+        adjoint(0)
     for i in range(4):
-        v = order[i]
-
         with phase("p_adj%d" % i):
-
-            @pl.loop(0, FT)
-            def _(ft, v=v):
-                re = pl.ds(pl.multiple_of(ft * LANES, LANES), LANES)
-                im = pl.ds(pl.multiple_of(NT + ft * LANES, LANES), LANES)
-                keep = lane + ft * LANES > 0
-                acc = [None] * (PD // 8)
-                for s in range(2 * SD):
-                    a = rh[ft, pl.ds(s * 4 + v, 8, stride=0), :]
-                    b = rh[FT + ft, pl.ds(s * 4 + v, 8, stride=0), :]
-                    ab = a + b
-                    for p in range(PD // 8):
-                        rows = pl.ds(p * 8, 8)
-                        terms = (a * kh[s, rows, re], b * kh[s, rows, im], ab * km[s, rows, re])
-                        acc[p] = terms if s == 0 else tuple(m + n for m, n in zip(acc[p], terms, strict=True))
-                for p in range(PD // 8):
-                    p1, p2, p3 = acc[p]
-                    grad[pl.ds(p * 8, 8), re] = jnp.where(keep, p1 + p2, p1)
-                    grad[pl.ds(p * 8, 8), im] = jnp.where(keep, p3 - p1 + p2, p2)
-
-        with phase("p_ainv%d" % i):
-            line_out[i] = matmul_t(stack(grad[...]), inverse)
+            if i < 3:
+                adjoint(i + 1)
+            line_out[i] = matmul_t(stack(grads[i % 2][...]), inverse)
         if i < 2:
             for j in range(SUB):
                 line_copy(i, j).start()
@@ -350,13 +370,12 @@
 def local(kernel, vectors, noise_scale, sensor_group, correlation, stiffness, couplings, neighbors):
     high, low = table()
     anywhere = pl.BlockSpec(memory_space=pl.ANY)
-    smem = pl.BlockSpec(memory_space=pltpu.SMEM)
     dma = pltpu.SemaphoreType.DMA
     count = len(PLANE)
     return pl.pallas_call(
         body,
         out_shape=jax.ShapeDtypeStruct((1, PD, NT), F32),
-        in_specs=[anywhere, anywhere, smem, smem] + [anywhere] * 6,
+        in_specs=[anywhere] * 10,
         out_specs=pl.BlockSpec(memory_space=pltpu.VMEM),
         scratch_shapes=[
             pltpu.VMEM((SD, PD, NT), F32),
@@ -367,6 +386,9 @@
             pltpu.VMEM((4, PD), jnp.int32),
             pltpu.VMEM((NT, F2), BF16),
             pltpu.VMEM((NT, F2), BF16),
+            pltpu.SMEM((SD,), F32),
+            pltpu.SMEM((SD,), jnp.int32),
+            pltpu.VMEM((2, SD * PD, 2 * NT), BF16),
             pltpu.VMEM((2 * SD, PD, F2), F32),
             pltpu.VMEM((2 * SD, PD, NT), F32),
             pltpu.VMEM((K, PD, F2), F32),
@@ -379,12 +401,13 @@
             pltpu.VMEM((16, 4, NT), F32),
             pltpu.VMEM((2 * FT, SD * K, LANES), F32),
             pltpu.VMEM((PD, F2), F32),
+            pltpu.VMEM((PD, F2), F32),
             pltpu.VMEM((PD, NT), F32),
             pltpu.VMEM((COLS, NT), F32),
             pltpu.VMEM((COLS, NT), F32),
             pltpu.VMEM((4, PD, NT), F32),
             pltpu.VMEM((4, PD, NT), F32),
-            dma((8,)),
+            dma((10,)),
             dma((2,)), dma((2,)),
             dma((count,)), dma((count,)),
             dma, dma,

time: 44 us -> 39.6 us (0.900)
  Pallas kernels: 42.3 us -> 37.9 us
    pallas_call x1, Pallas kernels: 42.3 us -> 37.9 us  [local(): pl.pallas_call(body, out_shape=jax.ShapeDtypeStruct((1, PD, NT), F32), in...]
where the time goes in v3:
time: 39.6 us; the launch traced here: 39.5 us
  Pallas kernels  37.9 us (96%)
  local copies, waits for them, and re-layouts  1.54 us (4%)
    pallas_call x1, Pallas kernels, local(): pl.pallas_call(body, out_shape=jax.ShapeDtypeStruct((1, PD, NT), F32), in...  37.9 us
    unnamed x1, local copies, waits for them, and re-layouts  1.54 us

profile of v3, /device:TPU:1, one launch (start us, length us, event | category | flops | bytes accessed | tf_op | source)
XLA Modules:
  0.0 39.5 jit_solution(12575685356930509393)
XLA Ops:
  0.0 37.9 %shard_map.100 = f32[1,64,384]{2,1,0:T(8,128)} custom-call(f32[8,64,384]{2,1,0:T(8,128)} %kern_hbm.1, f32[8,64,384]{2,1,0:T(8,128)} %vec_hbm.1, f32[8]{0:T(128)} %noise_hbm.1, s32[8]{0:T(128)} %group_hbm.1, f32[4,384,384]{2,1,0:T(8,128)} %corr_hbm.1, f32[1,64]{1,0:T(1,128)} %bitcast.1, f32[4,64]{1,0:T(4,128)} %coup_hbm.1, s32[4,64]{1,0:T(4,128)} %nbr_hbm.1, ...), custom_call_target="tpu_custom_call" | custom-call | tf_op jit(solution)/shard_map/pallas_call | solution.py:375
  37.9 1.5 %copy.12 = f32[1,64,384]{2,1,0:T(8,128)} copy(f32[1,64,384]{2,1,0:T(8,128)} %shard_map.100) | data formatting | bytes 196608

commit v4 on v3

v4 whole, which is shorter than its diff:
```python
import contextlib
import math

import jax
import jax.numpy as jnp
import numpy as np
from jax import lax
from jax.experimental import pallas as pl
from jax.experimental.pallas import tpu as pltpu
from jax.sharding import PartitionSpec as P

F32, BF16 = jnp.float32, jnp.bfloat16
phase = lambda name: contextlib.nullcontext()
K, NT, NB, SD, PD, COLS = 8, 384, 4, 8, 64, 16
F2 = 2 * NT
LANES = 128
FT = NT // LANES
VECTORS = (0, 2, 4, 6, 1, 3, 5, 7)
PIECES = ((0, 2), (2, 1))
RS_ORDER = ((2, 0), (2, 1), (1, 0), (3, 0), (1, 1), (3, 1), (0, 0), (0, 1))
PLANE = sorted(
    ((dx, dy) for dx in range(4) for dy in range(4) if dx or dy),
    key=lambda d: -(min(d[0], 4 - d[0]) + min(d[1], 4 - d[1])),
)


def table():
    t = np.arange(NT)
    angle = 2.0 * math.pi / F2 * (t[:, None] * t[None, :] % F2)
    second = -np.sin(angle)
    second[:, 0] = np.where(t % 2 == 0, 1.0, -1.0)
    parts = [np.cos(angle).reshape(NT, FT, 1, LANES), second.reshape(NT, FT, 1, LANES)]
    full = np.concatenate(parts, axis=2).reshape(NT, F2).astype(np.float32)
    high = full.astype(BF16)
    low = (full - high.astype(np.float32)).astype(BF16)
    return high, low


def split(x):
    high = x.astype(BF16)
    low = (x - high.astype(F32)).astype(BF16)
    return high, low


def stack(x):
    high, low = split(x)
    return jnp.concatenate([high, low, high], axis=1)


def matmul(a, b):
    return lax.dot_general(a, b, (((1,), (0,)), ((), ())), preferred_element_type=F32)


def matmul_t(a, b):
    return lax.dot_general(a, b, (((1,), (1,)), ((), ())), preferred_element_type=F32)


def body(
    kern_hbm, vec_hbm, noise_hbm, group_hbm, corr_hbm, stiff_hbm, coup_hbm, nbr_hbm, fh_hbm, fl_hbm,
    out_ref,
    kern, vec, corr, stiff, coup, nbr, fh, fl, noise, group, lhs, mix,
    kh, km, vh, ph, part, rs_in, zsum, z_in, mine, resid, rh, grad_a, grad_b, prior,
    halo_lo, halo_hi, line_out, line_in,
    load_sem, halo_send, halo_recv, rs_send, rs_recv, tell_send, tell_recv, z_send, z_recv, ag_send, ag_recv,
    share_send, share_recv, line_send, line_recv,
):
    pts, sens = lax.axis_index("pts"), lax.axis_index("sens")
    x, zh, y = pts % 4, pts // 4 % 2, pts // 8
    zl, core = sens // 2, sens % 2

    def plane(dx, dy):
        tx, ty = (x + dx) % 4, (y + dy) % 4
        return ty * 4 + tx, (ty * 2 + zh) * 4 + tx

    own_chunk = y * 4 + x
    z_peer = (y * 2 + 1 - zh) * 4 + x
    up, down = (pts + 1) % 32, (pts + 31) % 32
    core_peer = zl * 2 + 1 - core
    grads = (grad_a, grad_b)
    order = [3 - zl, (12 - 2 * zl) % 5, 3 - (12 - 2 * zl) % 5, zl]
    heads = [1 + zl % 2, order[1], order[2]]
    inner = zl * (3 - zl) // 2

    loads = [
        pltpu.make_async_copy(src, dst, load_sem.at[i])
        for i, (src, dst) in enumerate(
            [
                (kern_hbm, kern), (fh_hbm, fh), (fl_hbm, fl), (vec_hbm, vec), (corr_hbm, corr),
                (stiff_hbm, stiff), (coup_hbm, coup), (nbr_hbm, nbr), (noise_hbm, noise.at[0]), (group_hbm, group.at[0]),
            ]
        )
    ]
    for i in range(4):
        loads[i].start()

    barrier = pltpu.get_barrier_semaphore()
    greet = [{"pts": plane(dx, dy)[1]} for dx, dy in PLANE]
    greet += [{"pts": plane(dx, dy)[1], "sens": core_peer} for dx, dy in PLANE]
    greet += [{"pts": z_peer}, {"pts": up}, {"pts": down}, {"sens": core_peer}]
    greet += [{"sens": (zl + i) % 4 * 2 + core} for i in range(1, 4)]
    for target in greet:
        pl.semaphore_signal(barrier, inc=1, device_id=target, device_id_type=pl.DeviceIdType.MESH)

    def remote(src, dst, send, recv, target):
        return pltpu.make_async_remote_copy(
            src_ref=src, dst_ref=dst, send_sem=send, recv_sem=recv,
            device_id=target, device_id_type=pl.DeviceIdType.MESH,
        )

    freq = lax.broadcasted_iota(jnp.int32, (1, F2), 1)
    weight = jnp.where(freq * (freq - LANES) == 0, 1.0 / F2, 2.0 / F2).astype(F32)

    lane = lax.broadcasted_iota(jnp.int32, (8, LANES), 1)

    def columns(ft):
        return slice(ft * 2 * LANES, (ft + 1) * 2 * LANES)

    def parts(ft):
        return slice(ft * 2 * LANES, ft * 2 * LANES + LANES), slice(ft * 2 * LANES + LANES, (ft + 1) * 2 * LANES)

    def keep(ft, v, other):
        return jnp.where(lane > 0, v, other) if ft == 0 else v

    def hats(ft, i):
        which, first = i // 2, i % 2 * 4
        rows = slice(first * PD, (first + 4) * PD)
        a = jnp.concatenate([lhs[which, rows], lhs[which, rows, :NT]], axis=1)
        block = columns(ft)
        hat = matmul(a, jnp.concatenate([fh[:, block], fh[:, block], fl[:, block]], axis=0))
        if which == 0:
            hat = hat * weight[:, block]
            kh[first : first + 4, :, block] = hat.reshape(4, PD, 2 * LANES)
            km[first : first + 4, :, ft * LANES : (ft + 1) * LANES] = (hat[:, :LANES] - hat[:, LANES:]).reshape(4, PD, LANES)
        else:
            vh[first : first + 4, :, block] = hat.reshape(4, PD, 2 * LANES)

    def product(ft, i):
        re, im = parts(ft)
        s0 = 2 * i
        acc = [[None] * K for _ in range(6)]
        for p in range(PD // 8):
            rows = pl.ds(p * 8, 8)
            right = []
            for j in range(2):
                c, d = kh[s0 + j, rows, re], kh[s0 + j, rows, im]
                right.append((c, d, c + d))
            for k in range(K):
                a, b = vh[VECTORS[k], rows, re], vh[VECTORS[k], rows, im]
                left = (a, b, a + b)
                for j in range(2):
                    for q in range(3):
                        term = left[q] * right[j][q]
                        old = acc[j * 3 + q][k]
                        acc[j * 3 + q][k] = term if old is None else old + term
        for j in range(2):
            p1, p2, p3 = (
                jnp.concatenate([jnp.sum(v, axis=0, keepdims=True) for v in acc[j * 3 + q]], axis=0)
                for q in range(3)
            )
            rows = pl.ds((s0 + j) * 8, 8)
            ph[rows, re] = keep(ft, p1 - p2, p1)
            ph[rows, im] = keep(ft, p3 - p1 - p2, p2)

    def halve(which, rows):
        high, low = split(rows.reshape(SD * PD, NT))
        lhs[which, :, :NT] = high
        lhs[which, :, NT:] = low

    with phase("p_load"):
        loads[0].wait()
        halve(0, kern[...])
        loads[1].wait()
        loads[2].wait()
    for i in range(4, 10):
        loads[i].start()
    with phase("p_front0"):
        for i in range(2):
            hats(0, i)
        loads[3].wait()
        halve(1, vec[...])
        for i in range(2, 4):
            hats(0, i)
    with phase("p_front1"):
        for i in range(4):
            hats(1, i)
            product(0, i)
    with phase("p_front2"):
        for i in range(4):
            hats(2, i)
            product(1, i)
    with phase("p_front3"):
        for i in range(4):
            product(2, i)
    inverse = jnp.concatenate([fh[...], fh[...], fl[...]], axis=1)
    with phase("p_inv"):
        pred = matmul_t(stack(ph[...]), inverse)
        part[...] = pred.reshape(SD, K, NT)

    with phase("p_bar"):
        pl.semaphore_wait(barrier, len(greet))

    place = own_chunk
    theirs = place // SD
    rs, others = [], []
    distant = 1 - (y - 2 * core + 5) % 4 // 2
    for i, (dx, near) in enumerate(RS_ORDER):
        row, column = distant + near * (1 - 2 * distant), (x + dx) % 4
        s = row * 4 + column
        owner = core * SD + s
        target = {"pts": ((core * 2 + row) * 2 + zh) * 4 + column, "sens": zl * 2}
        rs.append(remote(part.at[s], rs_in.at[place], rs_send, rs_recv, target))
        others.append(core + (owner - place) * (owner - place) > 0)
        pl.when(others[i])(rs[i].start)

    halo = [
        remote(vec.at[sens, pl.ds(PD - COLS, COLS)], halo_lo, halo_send.at[0], halo_recv.at[0], {"pts": up}),
        remote(vec.at[sens, pl.ds(0, COLS)], halo_hi, halo_send.at[1], halo_recv.at[1], {"pts": down}),
    ]
    share = remote(kh.at[pl.ds(0, SD)], kh.at[pl.ds(SD, SD)], share_send, share_recv, {"sens": core_peer})
    for i in range(4, 10):
        loads[i].wait()
    tell = [
        remote(noise.at[0], noise.at[1], tell_send.at[0], tell_recv.at[0], {"sens": core_peer}),
        remote(group.at[0], group.at[1], tell_send.at[1], tell_recv.at[1], {"sens": core_peer}),
    ]
    for copy in tell + halo + [share]:
        copy.start()
    for copy in tell:
        copy.wait_recv()

    swap = remote(zsum, z_in, z_send, z_recv, {"pts": z_peer})
    ag = []
    for h in range(2):
        home = resid.at[place % SD + SD * ((theirs + h) % 2)]
        for i, (dx, dy) in enumerate(PLANE):
            target = {"pts": plane(dx, dy)[1], "sens": zl * 2 + h}
            ag.append(remote(mine.at[h], home, ag_send.at[h], ag_recv, target))
    ag.append(remote(mine.at[1], home, ag_send.at[1], ag_recv, {"sens": core_peer}))

    @pl.when(core == 0)
    def _():
        seat = lax.broadcasted_iota(jnp.int32, (1, SD), 1) == place % SD
        scale = jnp.sum(jnp.where(seat, jnp.where(theirs == 0, noise[0], noise[1]), 0.0), axis=1, keepdims=True)
        kind = jnp.sum(jnp.where(seat, jnp.where(theirs == 0, group[0], group[1]), 0), axis=1, keepdims=True)
        matrix = corr[0]
        for g in range(1, NB):
            matrix = jnp.where(kind == g, corr[g], matrix)
        mix_high, mix_low = split(matrix)
        mix[:, :NT] = mix_high
        mix[:, NT : 2 * NT] = mix_high
        mix[:, 2 * NT :] = mix_low

        @pl.when(theirs == 0)
        def _():
            rs_in[place] = part[place % SD]

        with phase("p_rswait"):
            for count in (15, 16):

                @pl.when(theirs == count - 15)
                def _(count=count):
                    rows = rs_in.at[pl.ds(0, count)]
                    remote(rows, rows, rs_send, rs_recv, {"pts": up}).wait_recv()

            total = rs_in[0]
            for i in range(1, 16):
                total = total + rs_in[i]
        zsum[...] = total
        swap.start()
        with phase("p_zwait"):
            swap.wait_recv()
        total = zsum[...] + z_in[...]
        tall = jnp.concatenate([total, jnp.zeros((8, NT), F32)], axis=0)
        value = scale * (total + matmul_t(stack(tall), mix[...])[:K])
        mine[0] = value[:4]
        mine[1] = value[4:]
        for copy in ag:
            copy.start()
        resid[place % SD + SD * theirs] = value[:4]

    with phase("p_prior"):
        for copy in halo:
            copy.wait_recv()
        q = lax.broadcasted_iota(jnp.int32, (PD + 2 * COLS, PD), 0)
        here = lax.broadcasted_iota(jnp.int32, (PD + 2 * COLS, PD), 1) + COLS
        local = nbr[...] - pts * PD + COLS
        links = coup[...]
        diagonal = stiff[...] + jnp.sum(links, axis=0, keepdims=True)
        pick = jnp.where(q == here, diagonal, 0.0)
        for j in range(4):
            pick = pick - jnp.where(q == local[j : j + 1], links[j : j + 1], 0.0)
        padded = jnp.concatenate([halo_lo[...], vec[sens], halo_hi[...]], axis=0)
        term = lax.dot_general(
            pick, padded, (((0,), (0,)), ((), ())),
            precision=lax.Precision.HIGHEST, preferred_element_type=F32,
        )
        for c in range(FT):
            prior[c] = term[:, c * LANES : (c + 1) * LANES]

    with phase("p_share"):
        share.wait_recv()
        for s in range(SD, 2 * SD):
            for ft in range(FT):
                re, im = parts(ft)
                km[s, :, ft * LANES : (ft + 1) * LANES] = kh[s, :, re] - kh[s, :, im]

    with phase("p_agwait"):
        for count in (15, 16):

            @pl.when(core == count - 15)
            def _(count=count):
                rows = resid.at[pl.ds(0, count)]
                remote(rows, rows, ag_send.at[0], ag_recv, {"sens": core_peer}).wait_recv()

    def line_copy(i, j):
        seat = 3 * (1 - inner) if i == 0 else i
        arrival = (1 - inner) * (3 + j) if i == 0 else i
        return remote(
            line_out.at[i, j], line_in.at[seat, j], line_send.at[i], line_recv.at[arrival],
            {"sens": heads[i] * 2 + core},
        )

    def line_arrival(i):
        return remote(line_in.at[i], line_in.at[i], line_send.at[0], line_recv.at[i], {"sens": core_peer})

    def adjoint(i, fts=tuple(range(FT))):
        v, into = order[i], grads[i % 2]
        for ft in fts:
            re, im = parts(ft)
            acc = [None] * (PD // 8)
            for s in range(2 * SD):
                a = rh[2 * ft, pl.ds(s * 4 + v, 8, stride=0), :]
                b = rh[2 * ft + 1, pl.ds(s * 4 + v, 8, stride=0), :]
                ab = a + b
                for p in range(PD // 8):
                    rows = pl.ds(p * 8, 8)
                    terms = (a * kh[s, rows, re], b * kh[s, rows, im], ab * km[s, rows, ft * LANES : (ft + 1) * LANES])
                    acc[p] = terms if s == 0 else tuple(m + n for m, n in zip(acc[p], terms, strict=True))
            for p in range(PD // 8):
                p1, p2, p3 = acc[p]
                into[pl.ds(p * 8, 8), re] = keep(ft, p1 + p2, p1)
                into[pl.ds(p * 8, 8), im] = keep(ft, p3 - p1 + p2, p2)

    with phase("p_adj0"):
        rows = stack(jnp.concatenate([resid[c] for c in range(2 * SD)], axis=0))
        for ft in range(FT):
            block = columns(ft)
            hat = matmul(rows, jnp.concatenate([fh[:, block], fh[:, block], fl[:, block]], axis=0))
            rh[2 * ft] = hat[:, :LANES]
            rh[2 * ft + 1] = hat[:, LANES:]
            adjoint(0, (ft,))
    for i in range(4):
        with phase("p_inv%d" % i):
            left = stack(grads[i % 2][...])
            for start, size in PIECES:
                data = matmul_t(left, inverse[start * LANES : (start + size) * LANES])
                for c in range(size):
                    line_out[i, start + c] = data[:, c * LANES : (c + 1) * LANES]
                    if i < 2:
                        line_copy(i, start + c).start()
            if i == 2:

                @pl.when(inner == 0)
                def _():
                    for j in range(FT):
                        line_copy(2, j).start()

        if i < 3:
            with phase("p_adj%d" % (i + 1)):

                @pl.when(core >= 0)
                def _(i=i):
                    adjoint(i + 1)

    with phase("p_relay"):

        @pl.when(inner == 1)
        def _():
            for j in range(FT):
                remote(line_in.at[3, j], line_in.at[3, j], line_send.at[0], line_recv.at[3 + j], {"sens": core_peer}).wait_recv()
                line_out[2, j] = line_out[2, j] + line_in[3, j]
                line_copy(2, j).start()

    prior[...] = prior[...] + line_out[3]

    with phase("p_linewait"):

        @pl.when(inner == 1)
        def _():
            with phase("p_lw0"):
                line_arrival(0).wait_recv()
            prior[...] = prior[...] + line_in[0]

        for i in (1, 2):
            with phase("p_lw%d" % i):
                line_arrival(i).wait_recv()
        for c in range(FT):
            out_ref[0, :, c * LANES : (c + 1) * LANES] = prior[c] + line_in[1, c] + line_in[2, c]

    with phase("p_sends"):
        for copy in halo + tell + [share]:
            copy.wait_send()
        for i in range(3):
            remote(line_out.at[i], line_out.at[i], line_send.at[i], line_recv.at[0], {"sens": core_peer}).wait_send()
        for count in (7, 8):

            @pl.when((core + theirs > 0) == (count == 8))
            def _(count=count):
                rows = part.at[pl.ds(0, count)]
                remote(rows, rows, rs_send, rs_recv, {"pts": up}).wait_send()

        @pl.when(core == 0)
        def _():
            swap.wait_send()
            for h in range(2):
                rows = resid.at[pl.ds(0, 15 + h)]
                remote(rows, rows, ag_send.at[h], ag_recv, {"sens": core_peer}).wait_send()


def local(kernel, vectors, noise_scale, sensor_group, correlation, stiffness, couplings, neighbors):
    high, low = table()
    anywhere = pl.BlockSpec(memory_space=pl.ANY)
    dma = pltpu.SemaphoreType.DMA
    return pl.pallas_call(
        body,
        out_shape=pltpu.VMEM((1, PD, NT), F32),
        in_specs=[anywhere] * 10,
        out_specs=pl.BlockSpec(memory_space=pltpu.VMEM),
        scratch_shapes=[
            pltpu.VMEM((SD, PD, NT), F32),
            pltpu.VMEM((K, PD, NT), F32),
            pltpu.VMEM((NB, NT, NT), F32),
            pltpu.VMEM((1, PD), F32),
            pltpu.VMEM((4, PD), F32),
            pltpu.VMEM((4, PD), jnp.int32),
            pltpu.VMEM((NT, F2), BF16),
            pltpu.VMEM((NT, F2), BF16),
            pltpu.VMEM((2, 1, SD), F32),
            pltpu.VMEM((2, 1, SD), jnp.int32),
            pltpu.VMEM((2, SD * PD, 2 * NT), BF16),
            pltpu.VMEM((NT, 3 * NT), BF16),
            pltpu.VMEM((2 * SD, PD, F2), F32),
            pltpu.VMEM((2 * SD, PD, NT), F32),
            pltpu.VMEM((K, PD, F2), F32),
            pltpu.VMEM((SD * K, F2), F32),
            pltpu.VMEM((SD, K, NT), F32),
            pltpu.VMEM((16, K, NT), F32),
            pltpu.VMEM((K, NT), F32),
            pltpu.VMEM((K, NT), F32),
            pltpu.VMEM((2, 4, NT), F32),
            pltpu.VMEM((16, 4, NT), F32),
            pltpu.VMEM((2 * FT, SD * K, LANES), F32),
            pltpu.VMEM((PD, F2), F32),
            pltpu.VMEM((PD, F2), F32),
            pltpu.VMEM((FT, PD, LANES), F32),
            pltpu.VMEM((COLS, NT), F32),
            pltpu.VMEM((COLS, NT), F32),
            pltpu.VMEM((4, FT, PD, LANES), F32),
            pltpu.VMEM((4, FT, PD, LANES), F32),
            dma((10,)),
            dma((2,)), dma((2,)),
            dma, dma,
            dma((2,)), dma((2,)),
            dma, dma,
            dma((2,)), dma,
            dma, dma,
            dma((3,)), dma((3 + FT,)),
        ],
        compiler_params=pltpu.CompilerParams(collective_id=0, has_side_effects=True),
    )(
        kernel, vectors, noise_scale.reshape(1, SD), sensor_group.reshape(1, SD), correlation, stiffness.reshape(1, PD),
        couplings, neighbors, jnp.asarray(high), jnp.asarray(low),
    )


def solution(mesh):
    in_specs = (
        P("sens", "pts", None),
        P(None, "pts", None),
        P("sens"),
        P("sens"),
        P(),
        P("pts"),
        P(None, "pts"),
        P(None, "pts"),
    )
    return jax.shard_map(
        local, mesh=mesh, in_specs=in_specs, out_specs=P("sens", "pts", None), check_vma=False
    )
```

time: 39.6 us -> 38.4 us (0.970)
  local copies, waits for them, and re-layouts: 1.54 us -> 0.64 us
    unnamed x1, local copies, waits for them, and re-layouts: 1.54 us -> 0.64 us
where the time goes in v4:
time: 38.4 us; the launch traced here: 38.3 us
  Pallas kernels  37.7 us (98%)
  local copies, waits for them, and re-layouts  0.64 us (2%)
    pallas_call x1, Pallas kernels, local(): pl.pallas_call(body, out_shape=pltpu.VMEM((1, PD, NT), F32), in_specs=[an...  37.7 us

profile of v4, /device:TPU:1, one launch (start us, length us, event | category | flops | bytes accessed | tf_op | source)
XLA Modules:
  0.0 38.3 jit_solution(16993202786297231340)
XLA Ops:
  0.0 37.7 %shard_map.100 = f32[1,64,384]{2,1,0:T(8,128)S(1)} custom-call(f32[8,64,384]{2,1,0:T(8,128)} %kern_hbm.1, f32[8,64,384]{2,1,0:T(8,128)} %vec_hbm.1, f32[1,8]{1,0:T(1,128)} %bitcast.3, s32[1,8]{1,0:T(1,128)} %bitcast.4, f32[4,384,384]{2,1,0:T(8,128)} %corr_hbm.1, f32[1,64]{1,0:T(1,128)} %bitcast.5, f32[4,64]{1,0:T(4,128)} %coup_hbm.1, s32[4,64]{1,0:T(4,128)} %nbr_hbm.1, ...), custom_call_target="tpu_custom_call" | custom-call | tf_op jit(solution)/shard_map/pallas_call | solution.py:424
  37.7 0.6 %copy.12 = f32[1,64,384]{2,1,0:T(8,128)} copy(f32[1,64,384]{2,1,0:T(8,128)S(1)} %shard_map.100) | data formatting | bytes 196608

commit v5 on v4

--- a/solution.py
+++ b/solution.py
@@ -16,7 +16,6 @@
 LANES = 128
 FT = NT // LANES
 VECTORS = (0, 2, 4, 6, 1, 3, 5, 7)
-PIECES = ((0, 2), (2, 1))
 RS_ORDER = ((2, 0), (2, 1), (1, 0), (3, 0), (1, 1), (3, 1), (0, 0), (0, 1))
 PLANE = sorted(
     ((dx, dy) for dx in range(4) for dy in range(4) if dx or dy),
@@ -29,11 +28,12 @@
     angle = 2.0 * math.pi / F2 * (t[:, None] * t[None, :] % F2)
     second = -np.sin(angle)
     second[:, 0] = np.where(t % 2 == 0, 1.0, -1.0)
-    parts = [np.cos(angle).reshape(NT, FT, 1, LANES), second.reshape(NT, FT, 1, LANES)]
-    full = np.concatenate(parts, axis=2).reshape(NT, F2).astype(np.float32)
+    blocks = np.stack([np.cos(angle).reshape(NT, FT, LANES), second.reshape(NT, FT, LANES)], axis=2)
+    full = blocks.reshape(NT, FT, 2 * LANES).transpose(1, 0, 2).astype(np.float32)
     high = full.astype(BF16)
     low = (full - high.astype(np.float32)).astype(BF16)
-    return high, low
+    both = np.stack([high, low], axis=1)
+    return both, np.ascontiguousarray(both.transpose(0, 1, 3, 2))
 
 
 def split(x):
@@ -56,13 +56,13 @@
 
 
 def body(
-    kern_hbm, vec_hbm, noise_hbm, group_hbm, corr_hbm, stiff_hbm, coup_hbm, nbr_hbm, fh_hbm, fl_hbm,
+    kern_hbm, vec_hbm, noise_hbm, group_hbm, corr_hbm, stiff_hbm, coup_hbm, nbr_hbm, fwd_hbm, inv_hbm,
     out_ref,
-    kern, vec, corr, stiff, coup, nbr, fh, fl, noise, group, lhs, mix,
+    kern, vec, corr, stiff, coup, nbr, fwd, inv, noise, group, lhs, mix,
     kh, km, vh, ph, part, rs_in, zsum, z_in, mine, resid, rh, grad_a, grad_b, prior,
-    halo_lo, halo_hi, line_out, line_in,
+    halo_lo, halo_hi, line_out, line_in, aid, aid_out,
     load_sem, halo_send, halo_recv, rs_send, rs_recv, tell_send, tell_recv, z_send, z_recv, ag_send, ag_recv,
-    share_send, share_recv, line_send, line_recv,
+    share_send, share_recv, line_send, line_recv, aid_recv,
 ):
     pts, sens = lax.axis_index("pts"), lax.axis_index("sens")
     x, zh, y = pts % 4, pts // 4 % 2, pts // 8
@@ -85,19 +85,21 @@
         pltpu.make_async_copy(src, dst, load_sem.at[i])
         for i, (src, dst) in enumerate(
             [
-                (kern_hbm, kern), (fh_hbm, fh), (fl_hbm, fl), (vec_hbm, vec), (corr_hbm, corr),
+                (kern_hbm.at[pl.ds(0, 4)], kern.at[pl.ds(0, 4)]), (fwd_hbm.at[0], fwd.at[0]),
+                (kern_hbm.at[pl.ds(4, 4)], kern.at[pl.ds(4, 4)]), (fwd_hbm.at[pl.ds(1, 2)], fwd.at[pl.ds(1, 2)]),
+                (vec_hbm, vec), (inv_hbm, inv), (corr_hbm, corr),
                 (stiff_hbm, stiff), (coup_hbm, coup), (nbr_hbm, nbr), (noise_hbm, noise.at[0]), (group_hbm, group.at[0]),
             ]
         )
     ]
-    for i in range(4):
+    for i in range(5):
         loads[i].start()
 
     barrier = pltpu.get_barrier_semaphore()
     greet = [{"pts": plane(dx, dy)[1]} for dx, dy in PLANE]
     greet += [{"pts": plane(dx, dy)[1], "sens": core_peer} for dx, dy in PLANE]
     greet += [{"pts": z_peer}, {"pts": up}, {"pts": down}, {"sens": core_peer}]
-    greet += [{"sens": (zl + i) % 4 * 2 + core} for i in range(1, 4)]
+    greet += [{"sens": (zl + i) % 4 * 2 + c} for i in range(1, 4) for c in (core, 1 - core)]
     for target in greet:
         pl.semaphore_signal(barrier, inc=1, device_id=target, device_id_type=pl.DeviceIdType.MESH)
 
@@ -118,6 +120,12 @@
     def parts(ft):
         return slice(ft * 2 * LANES, ft * 2 * LANES + LANES), slice(ft * 2 * LANES + LANES, (ft + 1) * 2 * LANES)
 
+    def forward(ft):
+        return jnp.concatenate([fwd[ft, 0], fwd[ft, 0], fwd[ft, 1]], axis=0)
+
+    def inverse(v, ft):
+        return matmul(stack(v), jnp.concatenate([inv[ft, 0], inv[ft, 0], inv[ft, 1]], axis=0))
+
     def keep(ft, v, other):
         return jnp.where(lane > 0, v, other) if ft == 0 else v
 
@@ -126,7 +134,7 @@
         rows = slice(first * PD, (first + 4) * PD)
         a = jnp.concatenate([lhs[which, rows], lhs[which, rows, :NT]], axis=1)
         block = columns(ft)
-        hat = matmul(a, jnp.concatenate([fh[:, block], fh[:, block], fl[:, block]], axis=0))
+        hat = matmul(a, forward(ft))
         if which == 0:
             hat = hat * weight[:, block]
             kh[first : first + 4, :, block] = hat.reshape(4, PD, 2 * LANES)
@@ -161,39 +169,50 @@
             ph[rows, re] = keep(ft, p1 - p2, p1)
             ph[rows, im] = keep(ft, p3 - p1 - p2, p2)
 
-    def halve(which, rows):
-        high, low = split(rows.reshape(SD * PD, NT))
-        lhs[which, :, :NT] = high
-        lhs[which, :, NT:] = low
+    def halve(which, first, rows):
+        high, low = split(rows.reshape(-1, NT))
+        lhs[which, first : first + high.shape[0], :NT] = high
+        lhs[which, first : first + high.shape[0], NT:] = low
 
     with phase("p_load"):
         loads[0].wait()
-        halve(0, kern[...])
+        halve(0, 0, kern[0:4])
         loads[1].wait()
+    with phase("p_front0"):
+        hats(0, 0)
         loads[2].wait()
-    for i in range(4, 10):
-        loads[i].start()
-    with phase("p_front0"):
-        for i in range(2):
-            hats(0, i)
+        halve(0, 4 * PD, kern[4:8])
+        hats(0, 1)
         loads[3].wait()
-        halve(1, vec[...])
-        for i in range(2, 4):
-            hats(0, i)
+        loads[4].wait()
+        for i in range(5, 12):
+            loads[i].start()
+        halve(1, 0, vec[...])
+        hats(1, 0)
+        hats(1, 1)
+        hats(0, 2)
+        hats(0, 3)
     with phase("p_front1"):
-        for i in range(4):
-            hats(1, i)
+        for i, (ft, rows) in enumerate(((1, 2), (1, 3), (2, 0), (2, 1))):
+            hats(ft, rows)
             product(0, i)
+    loads[5].wait()
     with phase("p_front2"):
-        for i in range(4):
-            hats(2, i)
-            product(1, i)
+        hats(2, 2)
+        product(1, 0)
+        product(1, 1)
+        hats(2, 3)
+        product(1, 2)
+        pred = inverse(ph[:, columns(0)], 0)
+        product(1, 3)
     with phase("p_front3"):
-        for i in range(4):
-            product(2, i)
-    inverse = jnp.concatenate([fh[...], fh[...], fl[...]], axis=1)
+        product(2, 0)
+        product(2, 1)
+        pred = pred + inverse(ph[:, columns(1)], 1)
+        product(2, 2)
+        product(2, 3)
     with phase("p_inv"):
-        pred = matmul_t(stack(ph[...]), inverse)
+        pred = pred + inverse(ph[:, columns(2)], 2)
         part[...] = pred.reshape(SD, K, NT)
 
     with phase("p_bar"):
@@ -217,7 +236,7 @@
         remote(vec.at[sens, pl.ds(0, COLS)], halo_hi, halo_send.at[1], halo_recv.at[1], {"pts": down}),
     ]
     share = remote(kh.at[pl.ds(0, SD)], kh.at[pl.ds(SD, SD)], share_send, share_recv, {"sens": core_peer})
-    for i in range(4, 10):
+    for i in range(6, 12):
         loads[i].wait()
     tell = [
         remote(noise.at[0], noise.at[1], tell_send.at[0], tell_recv.at[0], {"sens": core_peer}),
@@ -313,73 +332,88 @@
                 remote(rows, rows, ag_send.at[0], ag_recv, {"sens": core_peer}).wait_recv()
 
     def line_copy(i, j):
-        seat = 3 * (1 - inner) if i == 0 else i
-        arrival = (1 - inner) * (3 + j) if i == 0 else i
+        seat, arrival, to = i, i, core
+        if i == 0:
+            seat = (1 - inner) * (3 + core)
+            arrival = (1 - inner) * (3 + core * FT + j)
+            to = core * inner
         return remote(
-            line_out.at[i, j], line_in.at[seat, j], line_send.at[i], line_recv.at[arrival],
-            {"sens": heads[i] * 2 + core},
+            line_out.at[i, j], line_in.at[seat, j], line_send.at[i], line_recv.at[arrival], {"sens": heads[i] * 2 + to}
         )
+
+    assist = remote(line_out.at[2], aid, line_send.at[2], aid_recv, {"sens": core_peer})
 
     def line_arrival(i):
         return remote(line_in.at[i], line_in.at[i], line_send.at[0], line_recv.at[i], {"sens": core_peer})
 
-    def adjoint(i, fts=tuple(range(FT))):
+    def adjoint(i, ft):
         v, into = order[i], grads[i % 2]
-        for ft in fts:
-            re, im = parts(ft)
-            acc = [None] * (PD // 8)
-            for s in range(2 * SD):
-                a = rh[2 * ft, pl.ds(s * 4 + v, 8, stride=0), :]
-                b = rh[2 * ft + 1, pl.ds(s * 4 + v, 8, stride=0), :]
-                ab = a + b
-                for p in range(PD // 8):
-                    rows = pl.ds(p * 8, 8)
-                    terms = (a * kh[s, rows, re], b * kh[s, rows, im], ab * km[s, rows, ft * LANES : (ft + 1) * LANES])
-                    acc[p] = terms if s == 0 else tuple(m + n for m, n in zip(acc[p], terms, strict=True))
+        re, im = parts(ft)
+        acc = [None] * (PD // 8)
+        for s in range(2 * SD):
+            a = rh[2 * ft, pl.ds(s * 4 + v, 8, stride=0), :]
+            b = rh[2 * ft + 1, pl.ds(s * 4 + v, 8, stride=0), :]
+            ab = a + b
             for p in range(PD // 8):
-                p1, p2, p3 = acc[p]
-                into[pl.ds(p * 8, 8), re] = keep(ft, p1 + p2, p1)
-                into[pl.ds(p * 8, 8), im] = keep(ft, p3 - p1 + p2, p2)
-
-    with phase("p_adj0"):
-        rows = stack(jnp.concatenate([resid[c] for c in range(2 * SD)], axis=0))
-        for ft in range(FT):
-            block = columns(ft)
-            hat = matmul(rows, jnp.concatenate([fh[:, block], fh[:, block], fl[:, block]], axis=0))
-            rh[2 * ft] = hat[:, :LANES]
-            rh[2 * ft + 1] = hat[:, LANES:]
-            adjoint(0, (ft,))
+                rows = pl.ds(p * 8, 8)
+                terms = (a * kh[s, rows, re], b * kh[s, rows, im], ab * km[s, rows, ft * LANES : (ft + 1) * LANES])
+                acc[p] = terms if s == 0 else tuple(m + n for m, n in zip(acc[p], terms, strict=True))
+        for p in range(PD // 8):
+            p1, p2, p3 = acc[p]
+            into[pl.ds(p * 8, 8), re] = keep(ft, p1 + p2, p1)
+            into[pl.ds(p * 8, 8), im] = keep(ft, p3 - p1 + p2, p2)
+
+    def invert(i, ft):
+        return inverse(grads[i % 2][:, columns(ft)], ft)
+
     for i in range(4):
-        with phase("p_inv%d" % i):
-            left = stack(grads[i % 2][...])
-            for start, size in PIECES:
-                data = matmul_t(left, inverse[start * LANES : (start + size) * LANES])
-                for c in range(size):
-                    line_out[i, start + c] = data[:, c * LANES : (c + 1) * LANES]
-                    if i < 2:
-                        line_copy(i, start + c).start()
-            if i == 2:
-
-                @pl.when(inner == 0)
-                def _():
-                    for j in range(FT):
-                        line_copy(2, j).start()
-
-        if i < 3:
-            with phase("p_adj%d" % (i + 1)):
-
-                @pl.when(core >= 0)
-                def _(i=i):
-                    adjoint(i + 1)
+        with phase("p_adj%d" % i):
+            if i == 0:
+                rows = stack(jnp.concatenate([resid[c] for c in range(2 * SD)], axis=0))
+
+                def spectrum(ft):
+                    hat = matmul(rows, forward(ft))
+                    rh[2 * ft] = hat[:, :LANES]
+                    rh[2 * ft + 1] = hat[:, LANES:]
+
+                spectrum(0)
+                spectrum(1)
+            adjoint(i, 0)
+            if i == 0:
+                spectrum(2)
+            adjoint(i, 1)
+            data = invert(i, 0)
+            adjoint(i, 2)
+            data = data + invert(i, 1)
+            data = data + invert(i, 2)
+            for c in range(FT):
+                line_out[i, c] = data[:, c * LANES : (c + 1) * LANES]
+                if i < 2:
+                    line_copy(i, c).start()
+        if i == 2:
+
+            @pl.when(core * inner == 1)
+            def _():
+                assist.start()
+
+            @pl.when(inner == 0)
+            def _():
+                for j in range(FT):
+                    line_copy(2, j).start()
 
     with phase("p_relay"):
 
-        @pl.when(inner == 1)
+        @pl.when((1 - core) * inner == 1)
         def _():
+            assist.wait_recv()
             for j in range(FT):
-                remote(line_in.at[3, j], line_in.at[3, j], line_send.at[0], line_recv.at[3 + j], {"sens": core_peer}).wait_recv()
-                line_out[2, j] = line_out[2, j] + line_in[3, j]
-                line_copy(2, j).start()
+                for c, mine_out in ((0, line_out.at[2, j]), (1, aid_out.at[j])):
+                    came = line_in.at[3 + c, j]
+                    remote(came, came, line_send.at[0], line_recv.at[3 + c * FT + j], {"sens": core_peer}).wait_recv()
+                    mine_out[...] = came[...] + (aid[j] if c else line_out[2, j])
+                    remote(
+                        mine_out, line_in.at[2, j], line_send.at[2 + c], line_recv.at[2], {"sens": heads[2] * 2 + c}
+                    ).start()
 
     prior[...] = prior[...] + line_out[3]
 
@@ -412,13 +446,18 @@
         @pl.when(core == 0)
         def _():
             swap.wait_send()
+
+            @pl.when(inner == 1)
+            def _():
+                remote(aid_out, aid_out, line_send.at[3], line_recv.at[0], {"sens": core_peer}).wait_send()
+
             for h in range(2):
                 rows = resid.at[pl.ds(0, 15 + h)]
                 remote(rows, rows, ag_send.at[h], ag_recv, {"sens": core_peer}).wait_send()
 
 
 def local(kernel, vectors, noise_scale, sensor_group, correlation, stiffness, couplings, neighbors):
-    high, low = table()
+    ahead, back = table()
     anywhere = pl.BlockSpec(memory_space=pl.ANY)
     dma = pltpu.SemaphoreType.DMA
     return pl.pallas_call(
@@ -433,8 +472,8 @@
             pltpu.VMEM((1, PD), F32),
             pltpu.VMEM((4, PD), F32),
             pltpu.VMEM((4, PD), jnp.int32),
-            pltpu.VMEM((NT, F2), BF16),
-            pltpu.VMEM((NT, F2), BF16),
+            pltpu.VMEM((FT, 2, NT, 2 * LANES), BF16),
+            pltpu.VMEM((FT, 2, 2 * LANES, NT), BF16),
             pltpu.VMEM((2, 1, SD), F32),
             pltpu.VMEM((2, 1, SD), jnp.int32),
             pltpu.VMEM((2, SD * PD, 2 * NT), BF16),
@@ -456,20 +495,22 @@
             pltpu.VMEM((COLS, NT), F32),
             pltpu.VMEM((COLS, NT), F32),
             pltpu.VMEM((4, FT, PD, LANES), F32),
-            pltpu.VMEM((4, FT, PD, LANES), F32),
-            dma((10,)),
+            pltpu.VMEM((5, FT, PD, LANES), F32),
+            pltpu.VMEM((FT, PD, LANES), F32),
+            pltpu.VMEM((FT, PD, LANES), F32),
+            dma((12,)),
             dma((2,)), dma((2,)),
             dma, dma,
             dma((2,)), dma((2,)),
             dma, dma,
             dma((2,)), dma,
             dma, dma,
-            dma((3,)), dma((3 + FT,)),
+            dma((4,)), dma((3 + 2 * FT,)), dma,
         ],
         compiler_params=pltpu.CompilerParams(collective_id=0, has_side_effects=True),
     )(
         kernel, vectors, noise_scale.reshape(1, SD), sensor_group.reshape(1, SD), correlation, stiffness.reshape(1, PD),
-        couplings, neighbors, jnp.asarray(high), jnp.asarray(low),
+        couplings, neighbors, jnp.asarray(ahead), jnp.asarray(back),
     )
 
 

time: 38.4 us -> 38.6 us (level)
  no operation moved by 1% of the time
where the time goes in v5:
time: 38.6 us; the launch traced here: 38.5 us
  Pallas kernels  37.8 us (98%)
  local copies, waits for them, and re-layouts  0.64 us (2%)
    pallas_call x1, Pallas kernels, local(): pl.pallas_call(body, out_shape=pltpu.VMEM((1, PD, NT), F32), in_specs=[an...  37.8 us

profile of v5, /device:TPU:1, one launch (start us, length us, event | category | flops | bytes accessed | tf_op | source)
XLA Modules:
  0.0 38.5 jit_solution(11113462327884661877)
XLA Ops:
  0.0 37.8 %shard_map.100 = f32[1,64,384]{2,1,0:T(8,128)S(1)} custom-call(f32[8,64,384]{2,1,0:T(8,128)} %kern_hbm.1, f32[8,64,384]{2,1,0:T(8,128)} %vec_hbm.1, f32[1,8]{1,0:T(1,128)} %bitcast.3, s32[1,8]{1,0:T(1,128)} %bitcast.4, f32[4,384,384]{2,1,0:T(8,128)} %corr_hbm.1, f32[1,64]{1,0:T(1,128)} %bitcast.5, f32[4,64]{1,0:T(4,128)} %coup_hbm.1, s32[4,64]{1,0:T(4,128)} %nbr_hbm.1, ...), custom_call_target="tpu_custom_call" | custom-call | tf_op jit(solution)/shard_map/pallas_call | solution.py:463
  37.8 0.6 %copy.12 = f32[1,64,384]{2,1,0:T(8,128)} copy(f32[1,64,384]{2,1,0:T(8,128)S(1)} %shard_map.100) | data formatting | bytes 196608

commit v6 on v5

--- a/solution.py
+++ b/solution.py
@@ -16,6 +16,7 @@
 LANES = 128
 FT = NT // LANES
 VECTORS = (0, 2, 4, 6, 1, 3, 5, 7)
+TURNS = (((1, 0),), ((0, 0),), ((1, 1),), ((0, 1),))
 RS_ORDER = ((2, 0), (2, 1), (1, 0), (3, 0), (1, 1), (3, 1), (0, 0), (0, 1))
 PLANE = sorted(
     ((dx, dy) for dx in range(4) for dy in range(4) if dx or dy),
@@ -77,22 +78,24 @@
     up, down = (pts + 1) % 32, (pts + 31) % 32
     core_peer = zl * 2 + 1 - core
     grads = (grad_a, grad_b)
-    order = [3 - zl, (12 - 2 * zl) % 5, 3 - (12 - 2 * zl) % 5, zl]
-    heads = [1 + zl % 2, order[1], order[2]]
-    inner = zl * (3 - zl) // 2
+    is0, is3 = (3 - zl) // 3, zl // 3
+    is1 = zl % 2 - is3
+    is2 = 1 - is0 - is1 - is3
+    inner = is1 + is2
+    order = [3 * is0 + is2, 2 * is0 + 2 * is1 + 3 * is2 + 2 * is3, is0 + 3 * is1 + is3, zl]
+    heads = [is0 + is2 + 2 * is3, order[1], order[2]]
 
     loads = [
         pltpu.make_async_copy(src, dst, load_sem.at[i])
         for i, (src, dst) in enumerate(
             [
-                (kern_hbm.at[pl.ds(0, 4)], kern.at[pl.ds(0, 4)]), (fwd_hbm.at[0], fwd.at[0]),
-                (kern_hbm.at[pl.ds(4, 4)], kern.at[pl.ds(4, 4)]), (fwd_hbm.at[pl.ds(1, 2)], fwd.at[pl.ds(1, 2)]),
-                (vec_hbm, vec), (inv_hbm, inv), (corr_hbm, corr),
+                (kern_hbm, kern), (fwd_hbm.at[0], fwd.at[0]), (vec_hbm, vec),
+                (fwd_hbm.at[pl.ds(1, 2)], fwd.at[pl.ds(1, 2)]), (inv_hbm, inv), (corr_hbm, corr),
                 (stiff_hbm, stiff), (coup_hbm, coup), (nbr_hbm, nbr), (noise_hbm, noise.at[0]), (group_hbm, group.at[0]),
             ]
         )
     ]
-    for i in range(5):
+    for i in range(4):
         loads[i].start()
 
     barrier = pltpu.get_barrier_semaphore()
@@ -176,43 +179,32 @@
 
     with phase("p_load"):
         loads[0].wait()
-        halve(0, 0, kern[0:4])
+        halve(0, 0, kern[...])
         loads[1].wait()
     with phase("p_front0"):
-        hats(0, 0)
+        for i in range(2):
+            hats(0, i)
         loads[2].wait()
-        halve(0, 4 * PD, kern[4:8])
-        hats(0, 1)
         loads[3].wait()
-        loads[4].wait()
-        for i in range(5, 12):
+        for i in range(4, 11):
             loads[i].start()
         halve(1, 0, vec[...])
-        hats(1, 0)
-        hats(1, 1)
-        hats(0, 2)
-        hats(0, 3)
+        for i in range(2, 4):
+            hats(0, i)
     with phase("p_front1"):
-        for i, (ft, rows) in enumerate(((1, 2), (1, 3), (2, 0), (2, 1))):
-            hats(ft, rows)
+        for i in range(4):
+            hats(1, i)
             product(0, i)
-    loads[5].wait()
     with phase("p_front2"):
-        hats(2, 2)
-        product(1, 0)
-        product(1, 1)
-        hats(2, 3)
-        product(1, 2)
-        pred = inverse(ph[:, columns(0)], 0)
-        product(1, 3)
+        for i in range(4):
+            hats(2, i)
+            product(1, i)
+        loads[4].wait()
     with phase("p_front3"):
-        product(2, 0)
-        product(2, 1)
-        pred = pred + inverse(ph[:, columns(1)], 1)
-        product(2, 2)
-        product(2, 3)
+        for i in range(4):
+            product(2, i)
     with phase("p_inv"):
-        pred = pred + inverse(ph[:, columns(2)], 2)
+        pred = inverse(ph[:, columns(0)], 0) + inverse(ph[:, columns(1)], 1) + inverse(ph[:, columns(2)], 2)
         part[...] = pred.reshape(SD, K, NT)
 
     with phase("p_bar"):
@@ -236,7 +228,7 @@
         remote(vec.at[sens, pl.ds(0, COLS)], halo_hi, halo_send.at[1], halo_recv.at[1], {"pts": down}),
     ]
     share = remote(kh.at[pl.ds(0, SD)], kh.at[pl.ds(SD, SD)], share_send, share_recv, {"sens": core_peer})
-    for i in range(6, 12):
+    for i in range(5, 11):
         loads[i].wait()
     tell = [
         remote(noise.at[0], noise.at[1], tell_send.at[0], tell_recv.at[0], {"sens": core_peer}),
@@ -249,12 +241,13 @@
 
     swap = remote(zsum, z_in, z_send, z_recv, {"pts": z_peer})
     ag = []
-    for h in range(2):
+    for h in (0, 1):
         home = resid.at[place % SD + SD * ((theirs + h) % 2)]
         for i, (dx, dy) in enumerate(PLANE):
             target = {"pts": plane(dx, dy)[1], "sens": zl * 2 + h}
             ag.append(remote(mine.at[h], home, ag_send.at[h], ag_recv, target))
-    ag.append(remote(mine.at[1], home, ag_send.at[1], ag_recv, {"sens": core_peer}))
+        if h:
+            ag.append(remote(mine.at[1], home, ag_send.at[1], ag_recv, {"sens": core_peer}))
 
     @pl.when(core == 0)
     def _():
@@ -332,10 +325,10 @@
                 remote(rows, rows, ag_send.at[0], ag_recv, {"sens": core_peer}).wait_recv()
 
     def line_copy(i, j):
-        seat, arrival, to = i, i, core
+        seat, arrival, to = zl, zl, core
         if i == 0:
-            seat = (1 - inner) * (3 + core)
-            arrival = (1 - inner) * (3 + core * FT + j)
+            seat = inner * zl + (1 - inner) * (4 + core)
+            arrival = inner * zl + (1 - inner) * (4 + core * FT + j)
             to = core * inner
         return remote(
             line_out.at[i, j], line_in.at[seat, j], line_send.at[i], line_recv.at[arrival], {"sens": heads[i] * 2 + to}
@@ -388,13 +381,21 @@
             data = data + invert(i, 2)
             for c in range(FT):
                 line_out[i, c] = data[:, c * LANES : (c + 1) * LANES]
-                if i < 2:
-                    line_copy(i, c).start()
+
+        for when, which in TURNS[i]:
+
+            @pl.when(core == when)
+            def _(which=which):
+                for j in range(FT):
+                    line_copy(which, j).start()
+
         if i == 2:
 
             @pl.when(core * inner == 1)
             def _():
                 assist.start()
+
+        if i == 3:
 
             @pl.when(inner == 0)
             def _():
@@ -406,13 +407,14 @@
         @pl.when((1 - core) * inner == 1)
         def _():
             assist.wait_recv()
-            for j in range(FT):
-                for c, mine_out in ((0, line_out.at[2, j]), (1, aid_out.at[j])):
-                    came = line_in.at[3 + c, j]
-                    remote(came, came, line_send.at[0], line_recv.at[3 + c * FT + j], {"sens": core_peer}).wait_recv()
+            for c in (1, 0):
+                for j in range(FT):
+                    mine_out = aid_out.at[j] if c else line_out.at[2, j]
+                    came = line_in.at[4 + c, j]
+                    remote(came, came, line_send.at[0], line_recv.at[4 + c * FT + j], {"sens": core_peer}).wait_recv()
                     mine_out[...] = came[...] + (aid[j] if c else line_out[2, j])
                     remote(
-                        mine_out, line_in.at[2, j], line_send.at[2 + c], line_recv.at[2], {"sens": heads[2] * 2 + c}
+                        mine_out, line_in.at[zl, j], line_send.at[2 + c], line_recv.at[zl], {"sens": heads[2] * 2 + c}
                     ).start()
 
     prior[...] = prior[...] + line_out[3]
@@ -421,15 +423,19 @@
 
         @pl.when(inner == 1)
         def _():
-            with phase("p_lw0"):
-                line_arrival(0).wait_recv()
-            prior[...] = prior[...] + line_in[0]
-
-        for i in (1, 2):
-            with phase("p_lw%d" % i):
+            for i in (0, 3):
                 line_arrival(i).wait_recv()
-        for c in range(FT):
-            out_ref[0, :, c * LANES : (c + 1) * LANES] = prior[c] + line_in[1, c] + line_in[2, c]
+            prior[...] = prior[...] + line_in[0] + line_in[3]
+            line_arrival(3 - zl).wait_recv()
+            for c in range(FT):
+                out_ref[0, :, c * LANES : (c + 1) * LANES] = prior[c] + line_in[3 - zl, c]
+
+        @pl.when(inner == 0)
+        def _():
+            for i in (1, 2):
+                line_arrival(i).wait_recv()
+            for c in range(FT):
+                out_ref[0, :, c * LANES : (c + 1) * LANES] = prior[c] + line_in[1, c] + line_in[2, c]
 
     with phase("p_sends"):
         for copy in halo + tell + [share]:
@@ -495,17 +501,17 @@
             pltpu.VMEM((COLS, NT), F32),
             pltpu.VMEM((COLS, NT), F32),
             pltpu.VMEM((4, FT, PD, LANES), F32),
-            pltpu.VMEM((5, FT, PD, LANES), F32),
+            pltpu.VMEM((6, FT, PD, LANES), F32),
             pltpu.VMEM((FT, PD, LANES), F32),
             pltpu.VMEM((FT, PD, LANES), F32),
-            dma((12,)),
+            dma((11,)),
             dma((2,)), dma((2,)),
             dma, dma,
             dma((2,)), dma((2,)),
             dma, dma,
             dma((2,)), dma,
             dma, dma,
-            dma((4,)), dma((3 + 2 * FT,)), dma,
+            dma((4,)), dma((4 + 2 * FT,)), dma,
         ],
         compiler_params=pltpu.CompilerParams(collective_id=0, has_side_effects=True),
     )(

time: 38.6 us -> 37.7 us (0.977)
  the two profiles are of different devices: /device:TPU:1 before, /device:TPU:8 now
where the time goes in v6:
time: 37.7 us; the launch traced here: 37.6 us
  Pallas kernels  37 us (98%)
  local copies, waits for them, and re-layouts  0.64 us (2%)
    pallas_call x1, Pallas kernels, local(): pl.pallas_call(body, out_shape=pltpu.VMEM((1, PD, NT), F32), in_specs=[an...  37 us

profile of v6, /device:TPU:8, one launch (start us, length us, event | category | flops | bytes accessed | tf_op | source)
XLA Modules:
  0.0 37.6 jit_solution(12607920739607153118)
XLA Ops:
  0.0 37.0 %shard_map.100 = f32[1,64,384]{2,1,0:T(8,128)S(1)} custom-call(f32[8,64,384]{2,1,0:T(8,128)} %kern_hbm.1, f32[8,64,384]{2,1,0:T(8,128)} %vec_hbm.1, f32[1,8]{1,0:T(1,128)} %bitcast.3, s32[1,8]{1,0:T(1,128)} %bitcast.4, f32[4,384,384]{2,1,0:T(8,128)} %corr_hbm.1, f32[1,64]{1,0:T(1,128)} %bitcast.5, f32[4,64]{1,0:T(4,128)} %coup_hbm.1, s32[4,64]{1,0:T(4,128)} %nbr_hbm.1, ...), custom_call_target="tpu_custom_call" | custom-call | tf_op jit(solution)/shard_map/pallas_call | solution.py:469
  37.0 0.6 %copy.12 = f32[1,64,384]{2,1,0:T(8,128)} copy(f32[1,64,384]{2,1,0:T(8,128)S(1)} %shard_map.100) | data formatting | bytes 196608

commit v7 on v6

--- a/solution.py
+++ b/solution.py
@@ -366,8 +366,8 @@
 
                 def spectrum(ft):
                     hat = matmul(rows, forward(ft))
-                    rh[2 * ft] = hat[:, :LANES]
-                    rh[2 * ft + 1] = hat[:, LANES:]
+                    rh[2 * ft, : SD * K] = hat[:, :LANES]
+                    rh[2 * ft + 1, : SD * K] = hat[:, LANES:]
 
                 spectrum(0)
                 spectrum(1)
@@ -494,7 +494,7 @@
             pltpu.VMEM((K, NT), F32),
             pltpu.VMEM((2, 4, NT), F32),
             pltpu.VMEM((16, 4, NT), F32),
-            pltpu.VMEM((2 * FT, SD * K, LANES), F32),
+            pltpu.VMEM((2 * FT, SD * K + 8, LANES), F32),
             pltpu.VMEM((PD, F2), F32),
             pltpu.VMEM((PD, F2), F32),
             pltpu.VMEM((FT, PD, LANES), F32),

time: 37.7 us -> 37.7 us (level)
  no operation moved by 1% of the time
where the time goes in v7:
time: 37.7 us; the launch traced here: 37.6 us
  Pallas kernels  37 us (98%)
  local copies, waits for them, and re-layouts  0.64 us (2%)
    pallas_call x1, Pallas kernels, local(): pl.pallas_call(body, out_shape=pltpu.VMEM((1, PD, NT), F32), in_specs=[an...  37 us

profile of v7, /device:TPU:8, one launch (start us, length us, event | category | flops | bytes accessed | tf_op | source)
XLA Modules:
  0.0 37.6 jit_solution(6134721465159171561)
XLA Ops:
  0.0 37.0 %shard_map.100 = f32[1,64,384]{2,1,0:T(8,128)S(1)} custom-call(f32[8,64,384]{2,1,0:T(8,128)} %kern_hbm.1, f32[8,64,384]{2,1,0:T(8,128)} %vec_hbm.1, f32[1,8]{1,0:T(1,128)} %bitcast.3, s32[1,8]{1,0:T(1,128)} %bitcast.4, f32[4,384,384]{2,1,0:T(8,128)} %corr_hbm.1, f32[1,64]{1,0:T(1,128)} %bitcast.5, f32[4,64]{1,0:T(4,128)} %coup_hbm.1, s32[4,64]{1,0:T(4,128)} %nbr_hbm.1, ...), custom_call_target="tpu_custom_call" | custom-call | tf_op jit(solution)/shard_map/pallas_call | solution.py:469
  37.0 0.6 %copy.12 = f32[1,64,384]{2,1,0:T(8,128)} copy(f32[1,64,384]{2,1,0:T(8,128)S(1)} %shard_map.100) | data formatting | bytes 196608
